TPU v7x, 32 devices: a whole 2x2x4 slice. The times are simulated.
32 devices in a mesh: blk: 4 (over y, core), ulysses: 8 (over z, x).
Axes of the slice: x: 2, y: 2, z: 4, core: 2. Of those that a mesh axis runs over, the one named last changes fastest.
Arguments:
- query_tokens: bfloat16 [4096, 4096], P(('blk', 'ulysses')), may hold values from -5 to 5
- key_tokens: bfloat16 [4096, 4096], P(('blk', 'ulysses')), may hold values from -5 to 5
- value_tokens: bfloat16 [4096, 4096], P(('blk', 'ulysses')), may hold values from -5 to 5
- cotangent: bfloat16 [4096, 4096], P(('blk', 'ulysses')), may hold values from -5 to 5
- block_mask: int32 [32, 32], replicated, may hold values from 0 to 1, as said below
Outputs:
- attended: bfloat16 [4096, 4096], P(('blk', 'ulysses'))
- grad_query: bfloat16 [4096, 4096], P(('blk', 'ulysses'))
- grad_key: bfloat16 [4096, 4096], P(('blk', 'ulysses'))
- grad_value: bfloat16 [4096, 4096], P(('blk', 'ulysses'))
Inputs may be any that keep to these rules, and one draw needn't show every extreme that they name: block_mask is symmetric. A span is a run of 8 consecutive blocks. Inside a span, block s attends block s2 exactly when they differ by at most one. A query block attends at most one key block in each other span. The queries of one span attend keys of exactly 3 other spans, and at most 2 distinct key blocks of any other span; in every draw some pairs of spans reach 2.
All inputs are finite; a program needn't handle non-finite values.
Results may differ from a plain program's by a relative error of at most 0.0096.
Values may be sent and summed in bfloat16 or wider, within the bound.
No kernel may reach another device: no remote copies, remote signals or barrier semaphores. Data moves between devices by JAX's collectives and lax.ppermute only.
A program may use at most 128 MiB of HBM per device.

v0:
```python
import functools
import jax
import jax.numpy as jnp
from jax import lax
from jax.experimental import pallas as pl
from jax.experimental.pallas import tpu as pltpu
from jax.sharding import Mesh, PartitionSpec as P

HEAD_DIM = 128
BLOCK = 128
SUB = 2
NEG = float("-inf")
POS = float("inf")
BF16 = jnp.bfloat16
F32 = jnp.float32
SCALE = HEAD_DIM ** (-0.5)


def head_of(h):
    return slice(h * HEAD_DIM, (h + 1) * HEAD_DIM)


def dot_nt(a, b):
    return lax.dot_general(a, b, (((1,), (1,)), ((), ())), preferred_element_type=F32)


def dot_nn(a, b):
    return lax.dot_general(a, b, (((1,), (0,)), ((), ())), preferred_element_type=F32)


def pack_kernel(a_ref, b_ref, out_ref, held, in_sem, out_sem):
    groups, _, _, columns = out_ref.shape
    arrive, leave = [], []
    for c in range(groups):
        for n, source in enumerate((a_ref, b_ref)):
            arrive.append(
                pltpu.make_async_copy(
                    source.at[:, c * columns : (c + 1) * columns], held.at[c, n], in_sem.at[c, n]
                )
            )
            leave.append(pltpu.make_async_copy(held.at[c, n], out_ref.at[c, n], out_sem.at[c, n]))
    for copy in arrive:
        copy.start()
    for first, second in zip(arrive, leave):
        first.wait()
        second.start()
    for copy in leave:
        copy.wait()


def unpack_kernel(in_ref, a_ref, b_ref, held, in_sem, out_sem):
    groups, _, _, columns = in_ref.shape
    arrive, leave = [], []
    for c in range(groups):
        for n, target in enumerate((a_ref, b_ref)):
            arrive.append(pltpu.make_async_copy(in_ref.at[c, n], held.at[c, n], in_sem.at[c, n]))
            leave.append(
                pltpu.make_async_copy(
                    held.at[c, n], target.at[:, c * columns : (c + 1) * columns], out_sem.at[c, n]
                )
            )
    for copy in arrive:
        copy.start()
    for first, second in zip(arrive, leave):
        first.wait()
        second.start()
    for copy in leave:
        copy.wait()


def pack(a, b, groups):
    rows, columns = a.shape
    shape = (groups, 2, rows, columns // groups)
    anywhere = pl.BlockSpec(memory_space=pl.ANY)
    return pl.pallas_call(
        pack_kernel,
        out_shape=jax.ShapeDtypeStruct(shape, a.dtype),
        in_specs=[anywhere] * 2,
        out_specs=anywhere,
        scratch_shapes=[
            pltpu.VMEM(shape, a.dtype),
            pltpu.SemaphoreType.DMA((groups, 2)),
            pltpu.SemaphoreType.DMA((groups, 2)),
        ],
        name="pack",
    )(a, b)


def unpack(pair):
    groups, _, rows, columns = pair.shape
    anywhere = pl.BlockSpec(memory_space=pl.ANY)
    flat = jax.ShapeDtypeStruct((rows, groups * columns), pair.dtype)
    return pl.pallas_call(
        unpack_kernel,
        out_shape=(flat, flat),
        in_specs=[anywhere],
        out_specs=(anywhere, anywhere),
        scratch_shapes=[
            pltpu.VMEM(pair.shape, pair.dtype),
            pltpu.SemaphoreType.DMA((groups, 2)),
            pltpu.SemaphoreType.DMA((groups, 2)),
        ],
        name="unpack",
    )(pair)


def fill_pool(count, parts, pool, extra, which, sem, extra_sem):
    copies = []
    start = 0
    for m, source in enumerate(parts):
        size = source.shape[0]
        copies.append(pltpu.make_async_copy(source, pool.at[pl.ds(start, size)], sem.at[m]))
        start += size
    for copy in copies:
        copy.start()

    def move(slot):
        return pltpu.make_async_copy(extra.at[slot, which], pool.at[start + slot], extra_sem.at[slot])

    lax.fori_loop(0, count, lambda slot, _: (move(slot).start(), 0)[1], 0)
    for copy in copies:
        copy.wait()
    lax.fori_loop(0, count, lambda slot, _: (move(slot).wait(), 0)[1], 0)


def by_width(cross, width, body):
    narrow = min(4, width)
    if narrow == width:
        body(width)
        return

    @pl.when(cross < 2)
    def _():
        body(narrow)

    @pl.when(cross >= 2)
    def _():
        body(width)


def query_kernel(
    width, heads, slot_ref, valid_ref, cross_ref, count_ref, qg_ref, kv_local, below, above, extra,
    out_ref, stat_ref, pool, sem, extra_sem,
):
    fill_pool(count_ref[0], (kv_local, below, above), pool, extra, 0, sem, extra_sem)
    eye = lax.broadcasted_iota(jnp.int32, (BLOCK, BLOCK), 0) == lax.broadcasted_iota(
        jnp.int32, (BLOCK, BLOCK), 1
    )

    def to_row(column):
        return jnp.sum(jnp.where(eye, column, 0.0), axis=0, keepdims=True)

    def block(i, _):
        def body(count):
            slots = [slot_ref[i, t] for t in range(count)]
            bias = jnp.concatenate(
                [
                    jnp.full((1, BLOCK), jnp.where(valid_ref[i, t] > 0, 0.0, NEG), F32)
                    for t in range(count)
                ],
                axis=1,
            )
            for h in range(heads):
                cols = head_of(h)
                q = qg_ref[i, 0, :, cols]
                g = qg_ref[i, 1, :, cols]
                keys = jnp.concatenate([pool[s, 0, :, cols] for s in slots], axis=0)
                values = jnp.concatenate([pool[s, 1, :, cols] for s in slots], axis=0)
                scores = dot_nt(q, keys) * SCALE + bias
                peak = jnp.max(scores, axis=1, keepdims=True)
                prob = jnp.exp(scores - peak)
                total = jnp.sum(prob, axis=1, keepdims=True)
                prob = prob * (1.0 / total)
                out = dot_nn(prob.astype(BF16), values)
                delta = jnp.sum(g.astype(F32) * out, axis=1, keepdims=True)
                dprob = dot_nt(g, values)
                dscore = (prob * (dprob - delta)).astype(BF16)
                out_ref[i, 0, :, cols] = out.astype(BF16)
                out_ref[i, 1, :, cols] = (dot_nn(dscore, keys) * SCALE).astype(BF16)
                stat_ref[i, 0, pl.ds(h, 1), :] = to_row(peak + jnp.log(total))
                stat_ref[i, 1, pl.ds(h, 1), :] = to_row(delta)

        by_width(cross_ref[i], width, body)
        return 0

    lax.fori_loop(0, qg_ref.shape[0], block, 0)


def key_kernel(
    width, heads, slot_ref, valid_ref, place_ref, cross_ref, count_ref, kv_ref, stat_ref, qg_local,
    below, above, extra, out_ref, pool, sem, extra_sem,
):
    fill_pool(count_ref[0], (qg_local, below, above), pool, extra, 1, sem, extra_sem)

    def block(j, _):
        def body(count):
            slots = [slot_ref[j, t] for t in range(count)]
            places = [place_ref[j, t] for t in range(count)]
            for h in range(heads):
                cols = head_of(h)
                k = kv_ref[j, 0, :, cols]
                v = kv_ref[j, 1, :, cols]
                queries = jnp.concatenate([pool[s, 0, :, cols] for s in slots], axis=0)
                upstream = jnp.concatenate([pool[s, 1, :, cols] for s in slots], axis=0)
                log_row = jnp.concatenate(
                    [
                        jnp.where(valid_ref[j, t] > 0, stat_ref[places[t], 0, pl.ds(h, 1), :], POS)
                        for t in range(count)
                    ],
                    axis=1,
                )
                delta_row = jnp.concatenate(
                    [stat_ref[places[t], 1, pl.ds(h, 1), :] for t in range(count)], axis=1
                )
                prob = jnp.exp(dot_nt(k, queries) * SCALE - log_row)
                dprob = dot_nt(v, upstream)
                dscore = (prob * (dprob - delta_row)).astype(BF16)
                out_ref[j, 1, :, cols] = dot_nn(prob.astype(BF16), upstream).astype(BF16)
                out_ref[j, 0, :, cols] = (dot_nn(dscore, queries) * SCALE).astype(BF16)

        by_width(cross_ref[j], width, body)
        return 0

    lax.fori_loop(0, kv_ref.shape[0], block, 0)


def tables(block_mask, spans, span_len, steps):
    z = lax.axis_index("z")
    local = spans * SUB
    iota = functools.partial(lax.broadcasted_iota, jnp.int32)
    cube = block_mask.reshape(spans, span_len, spans, span_len)
    spot = iota(cube.shape, 3)
    partner = jnp.sum(cube * (spot + 1), axis=3) - 1
    shape = partner.shape
    mine, spot, other = iota(shape, 0), iota(shape, 1), iota(shape, 2)
    linked = (partner >= 0) & (mine != other)
    hop = jnp.where(linked, (partner // SUB) ^ (spot // SUB), 0)
    per_place = hop.reshape(spans, steps, SUB, spans)
    rounds = [
        jnp.max(jnp.sum((per_place == d).astype(jnp.int32), axis=(0, 2, 3))) for d in range(1, steps)
    ]
    key = jnp.where(
        mine < other,
        (mine * span_len + spot) * spans + other,
        (other * span_len + partner) * spans + mine,
    )

    def at_place(table):
        return lax.dynamic_slice_in_dim(table, z * SUB, SUB, 1).reshape(local, spans)

    partner_l, linked_l, hop_l, key_l = at_place(partner), at_place(linked), at_place(hop), at_place(key)
    other_l = at_place(other)
    block_l = iota((local, spans), 0)
    order = (hop_l * (spans * span_len * spans) + key_l).reshape(-1)
    crossing = (hop_l > 0).reshape(-1)
    earlier = crossing[None, :] & (order[None, :] < order[:, None])
    extra_slot = jnp.sum(earlier.astype(jnp.int32), axis=1)
    capacity = spans * (spans - 1)
    hits = crossing[:, None] & (extra_slot[:, None] == iota((local * spans, capacity), 1))
    send_block = jnp.sum(hits.astype(jnp.int32) * block_l.reshape(-1)[:, None], axis=0)
    counts = jnp.stack([jnp.sum((hop_l == d).astype(jnp.int32)) for d in range(1, steps)])
    count = jnp.sum(counts)
    cross_slot = jnp.where(
        hop_l > 0,
        local + 2 * spans + extra_slot.reshape(local, spans),
        other_l * SUB + partner_l % SUB,
    )
    cross_place = (partner_l // SUB) * local + other_l * SUB + partner_l % SUB
    own = block_l[:, :1]
    span_l, x_l = own // SUB, own % SUB
    left_slot = jnp.where(x_l > 0, own - 1, local + span_l)
    right_slot = jnp.where(x_l < SUB - 1, own + 1, local + spans + span_l)
    left_ok = (x_l > 0) | (z > 0)
    right_ok = (x_l < SUB - 1) | (z < steps - 1)
    own_place = z * local + own
    left_place = jnp.where(x_l > 0, own_place - 1, (z - 1) * local + span_l * SUB + SUB - 1)
    right_place = jnp.where(x_l < SUB - 1, own_place + 1, (z + 1) * local + span_l * SUB)
    before = iota((local, spans, spans), 2) < iota((local, spans, spans), 1)
    rank = jnp.sum((linked_l[:, None, :] & before).astype(jnp.int32), axis=2)
    chosen = linked_l[:, None, :] & (rank[:, None, :] == iota((local, spans - 1, spans), 1))

    def pick(table):
        return jnp.sum(jnp.where(chosen, table[:, None, :], 0), axis=2)

    ok = jnp.concatenate(
        [jnp.ones_like(own), left_ok.astype(jnp.int32), right_ok.astype(jnp.int32), pick(linked_l.astype(jnp.int32))],
        axis=1,
    )
    slot = jnp.where(ok > 0, jnp.concatenate([own, left_slot, right_slot, pick(cross_slot)], axis=1), own)
    place = jnp.where(
        ok > 0, jnp.concatenate([own_place, left_place, right_place, pick(cross_place)], axis=1), own_place
    )
    cross = jnp.sum(linked_l.astype(jnp.int32), axis=1)
    return slot, ok, place, cross, count, counts, rounds, send_block, capacity


def shards(query_tokens, key_tokens, value_tokens, cotangent, block_mask):
    spans = lax.axis_size("blk")
    steps = lax.axis_size("z")
    span_len = steps * SUB
    local = spans * SUB

    def exchange(pair):
        return lax.all_to_all(pair, ("blk", "x"), split_axis=0, concat_axis=0, tiled=True)

    kv = exchange(pack(key_tokens, value_tokens, local))
    qg = exchange(pack(query_tokens, cotangent, local))
    columns = kv.shape[3]
    heads = columns // HEAD_DIM
    slot, ok, place, cross, count, counts, rounds, send_block, capacity = tables(
        block_mask, spans, span_len, steps
    )
    width = slot.shape[1]
    upward = [(n, n + 1) for n in range(steps - 1)]
    downward = [(n + 1, n) for n in range(steps - 1)]

    def neighbours(pair):
        edges = pair.reshape(spans, SUB, 2, BLOCK, columns)
        below = lax.ppermute(edges[:, SUB - 1], "z", upward)
        above = lax.ppermute(edges[:, 0], "z", downward)
        return below, above

    kv_below, kv_above = neighbours(kv)
    qg_below, qg_above = neighbours(qg)

    extra = pl.pallas_call(
        lambda out_ref: None,
        out_shape=jax.ShapeDtypeStruct((capacity + 1, 2, 2, BLOCK, columns), BF16),
        out_specs=pl.BlockSpec(memory_space=pl.ANY),
        name="extra_blocks",
    )()
    first = jnp.int32(0)
    for d in range(1, steps):
        swap = [(n, n ^ d) for n in range(steps)]
        mine = counts[d - 1]

        def one_round(r, buffer, swap=swap, first=first, mine=mine):
            at = jnp.where(r < mine, first + r, capacity)
            start = send_block[jnp.minimum(at, capacity - 1)]
            sent = jnp.concatenate([lax.dynamic_slice_in_dim(t, start, 1, 0) for t in (kv, qg)])
            got = lax.ppermute(sent, "z", swap)
            return lax.dynamic_update_slice_in_dim(buffer, got[None], at, 0)

        extra = lax.fori_loop(0, rounds[d - 1], one_round, extra)
        first = first + mine
    count = count.reshape(1)

    smem = pl.BlockSpec(memory_space=pltpu.SMEM)
    vmem = pl.BlockSpec(memory_space=pltpu.VMEM)
    anywhere = pl.BlockSpec(memory_space=pl.ANY)
    scratch = [
        pltpu.VMEM((local + 2 * spans + capacity, 2, BLOCK, columns), BF16),
        pltpu.SemaphoreType.DMA((3,)),
        pltpu.SemaphoreType.DMA((capacity,)),
    ]
    cost = pl.CostEstimate(
        flops=2 * 4 * local * heads * width * BLOCK * BLOCK * HEAD_DIM,
        bytes_accessed=16 * local * BLOCK * columns,
        transcendentals=local * heads * width * BLOCK * BLOCK,
    )
    stat_shape = (local, 2, heads, BLOCK)
    out_pair, stats = pl.pallas_call(
        functools.partial(query_kernel, width, heads),
        out_shape=(
            jax.ShapeDtypeStruct(qg.shape, BF16),
            jax.ShapeDtypeStruct(stat_shape, F32),
        ),
        in_specs=[smem] * 4 + [vmem] + [anywhere] * 4,
        out_specs=(vmem, vmem),
        scratch_shapes=scratch,
        cost_estimate=cost,
        name="query_pass",
    )(slot, ok, cross, count, qg, kv, kv_below, kv_above, extra)
    spread = jnp.broadcast_to(stats[None], (steps,) + stats.shape)
    all_stats = lax.all_to_all(spread, "z", split_axis=0, concat_axis=0, tiled=True)
    all_stats = all_stats.reshape(steps * local, 2, heads, BLOCK)
    grad_pair = pl.pallas_call(
        functools.partial(key_kernel, width, heads),
        out_shape=jax.ShapeDtypeStruct(kv.shape, BF16),
        in_specs=[smem] * 5 + [vmem, vmem] + [anywhere] * 4,
        out_specs=vmem,
        scratch_shapes=scratch,
        cost_estimate=cost,
        name="key_pass",
    )(slot, ok, place, cross, count, kv, all_stats, qg, qg_below, qg_above, extra)
    attended, grad_query = unpack(exchange(out_pair))
    grad_key, grad_value = unpack(exchange(grad_pair))
    return attended, grad_query, grad_key, grad_value


def solution(mesh):
    spans, ulysses = mesh.shape["blk"], mesh.shape["ulysses"]
    split = Mesh(mesh.devices.reshape(spans, ulysses // SUB, SUB), ("blk", "z", "x"))
    tokens = P(("blk", "z", "x"), None)
    return jax.shard_map(
        shards,
        mesh=split,
        in_specs=(tokens, tokens, tokens, tokens, P()),
        out_specs=(tokens, tokens, tokens, tokens),
        check_vma=False,
    )
```

profile of v0, /device:TPU:0, one launch (start us, length us, event | category | flops | bytes accessed | tf_op | source)
XLA Modules:
  0.0 311.2 jit_solution(4405503535263716850)
XLA Ops:
  0.6 2.7 pack.3
  3.3 5.2 %all-to-all-start.1 = ((bf16[8,2,128,512]{3,2,1,0:T(8,128)(2,1)}), bf16[8,2,128,512]{3,2,1,0:T(8,128)(2,1)S(1)}, u32[]{:S(2)}, u32[]{:S(2)}) async-start(bf16[8,2,128,512]{3,2,1,0:T(8,128)(2,1)} %pack.3), calls=%async_computation.1 | async-start | bytes 4194304 | tf_op jit(solution)/shard_map/all_to_all | solution.py:304
  9.7 0.7 fusion.11
  11.0 0.6 reduce_max.27
  11.6 0.7 reduce_max.28
  12.5 0.6 reduce_max.29
  14.4 0.6 reduce_sum.165.cross_ref
  15.0 2.6 pack.2
  19.7 14.9 %all-to-all-done.1.kv_local.kv_ref = bf16[8,2,128,512]{3,2,1,0:T(8,128)(2,1)S(1)} async-done(((bf16[8,2,128,512]{3,2,1,0:T(8,128)(2,1)}), bf16[8,2,128,512]{3,2,1,0:T(8,128)(2,1)S(1)}, u32[]{:S(2)}, u32[]{:S(2)}) %all-to-all-start.1) | async-done | bytes 2097184 | tf_op jit(solution)/shard_map/all_to_all | solution.py:304
  34.6 4.4 %all-to-all-start = ((bf16[8,2,128,512]{3,2,1,0:T(8,128)(2,1)}), bf16[8,2,128,512]{3,2,1,0:T(8,128)(2,1)}, u32[]{:S(2)}, u32[]{:S(2)}) async-start(bf16[8,2,128,512]{3,2,1,0:T(8,128)(2,1)} %pack.2), calls=%async_computation | async-start | bytes 4194304 | tf_op jit(solution)/shard_map/all_to_all | solution.py:304
  39.1 0.7 add_select_fusion.4
  39.9 0.7 add_select_fusion.3.slot_ref
  40.6 1.5 slice_bitcast_fusion.2
  42.1 4.5 %collective-permute-start.3 = (bf16[4,2,128,512]{3,2,1,0:T(8,128)(2,1)}, bf16[4,2,128,512]{3,2,1,0:T(8,128)(2,1)}, u32[]{:S(2)}, u32[]{:S(2)}) collective-permute-start(bf16[4,2,128,512]{3,2,1,0:T(8,128)(2,1)} %get-tuple-element.220), channel_id=1, source_target_pairs={{0,2},{2,4},{4,6},{1,3},{3,5},{5,7},{8,10},{10,12},{12,14},{9,11},... | collective-permute-start | bytes 3145736 | tf_op jit(solution)/shard_map/ppermute | solution.py:319
  46.6 1.3 collective-permute-start.4
  47.9 17.2 %all-to-all-done.qg_ref.qg_local = bf16[8,2,128,512]{3,2,1,0:T(8,128)(2,1)} async-done(((bf16[8,2,128,512]{3,2,1,0:T(8,128)(2,1)}), bf16[8,2,128,512]{3,2,1,0:T(8,128)(2,1)}, u32[]{:S(2)}, u32[]{:S(2)}) %all-to-all-start) | async-done | bytes 2097184 | tf_op jit(solution)/shard_map/all_to_all | solution.py:304
  65.6 125.8 %while.31 = (s32[]{:T(128)}, bf16[13,2,2,128,512]{4,3,2,1,0:T(8,128)(2,1)}, s32[]{:T(128)}, s32[]{:T(128)}, s32[]{:T(128)}, /*index=5*/s32[12]{0:T(128)S(1)}, bf...) while((s32[]{:T(128)}, ...), condition=%wide.region_19.20_spmd, body=%wide.region_18.19_spmd.sunk | while | flops 262159 | bytes 5243221 | solution.py:344
  67.5 0.6 dynamic_slice.76
  70.1 1.0 constant_dynamic-slice_fusion.14
  71.1 2.7 collective-permute-start.1
  73.8 23.1 %collective-permute-done.1 = bf16[2,2,128,512]{3,2,1,0:T(8,128)(2,1)S(1)} collective-permute-done((bf16[2,2,128,512]{3,2,1,0:T(8,128)(2,1)S(1)}, bf16[2,2,128,512]{3,2,1,0:T(8,128)(2,1)S(1)}, u32[]{:S(2)}, u32[]{:S(2)}) %collective-permute-start.1) | collective-permute-done | bytes 524320 | tf_op jit(solution)/shard_map/while/body/ppermute | solution.py:341
  96.9 0.8 bitcast_dynamic-update-slice_fusion.7
  99.7 0.6 dynamic_slice.76
  102.2 1.0 constant_dynamic-slice_fusion.14
  103.4 24.9 %collective-permute-done.1 = bf16[2,2,128,512]{3,2,1,0:T(8,128)(2,1)S(1)} collective-permute-done((bf16[2,2,128,512]{3,2,1,0:T(8,128)(2,1)S(1)}, bf16[2,2,128,512]{3,2,1,0:T(8,128)(2,1)S(1)}, u32[]{:S(2)}, u32[]{:S(2)}) %collective-permute-start.1) | collective-permute-done | bytes 524320 | tf_op jit(solution)/shard_map/while/body/ppermute | solution.py:341
  128.3 0.8 bitcast_dynamic-update-slice_fusion.7
  133.7 1.0 constant_dynamic-slice_fusion.14
  134.8 24.1 %collective-permute-done.1 = bf16[2,2,128,512]{3,2,1,0:T(8,128)(2,1)S(1)} collective-permute-done((bf16[2,2,128,512]{3,2,1,0:T(8,128)(2,1)S(1)}, bf16[2,2,128,512]{3,2,1,0:T(8,128)(2,1)S(1)}, u32[]{:S(2)}, u32[]{:S(2)}) %collective-permute-start.1) | collective-permute-done | bytes 524320 | tf_op jit(solution)/shard_map/while/body/ppermute | solution.py:341
  158.9 0.8 bitcast_dynamic-update-slice_fusion.7
  161.7 0.6 dynamic_slice.76
  164.2 1.0 constant_dynamic-slice_fusion.14
  165.4 24.5 %collective-permute-done.1 = bf16[2,2,128,512]{3,2,1,0:T(8,128)(2,1)S(1)} collective-permute-done((bf16[2,2,128,512]{3,2,1,0:T(8,128)(2,1)S(1)}, bf16[2,2,128,512]{3,2,1,0:T(8,128)(2,1)S(1)}, u32[]{:S(2)}, u32[]{:S(2)}) %collective-permute-start.1) | collective-permute-done | bytes 524320 | tf_op jit(solution)/shard_map/while/body/ppermute | solution.py:341
  189.9 0.8 bitcast_dynamic-update-slice_fusion.7
  192.0 24.4 %query_pass.1 = (bf16[8,2,128,512]{3,2,1,0:T(8,128)(2,1)}, f32[8,2,4,128]{3,2,1,0:T(4,128)}) custom-call(s32[8,6]{1,0:T(8,128)} %add_select_fusion.3.slot_ref, s32[8,6]{1,0:T(8,128)} %get-tuple-element.200.valid_ref, s32[8]{0:T(128)} %reduce_sum.165.cross_ref, s32[1]{0:T(128)} %bitcast.7.count_ref, bf16[8,2,128,512]{3,2,1,0:T(8,128)(2,1)} %all-to-all-done.qg_ref.qg_local, ...), custom_call_target="tpu_custom_call" | custom-call | flops 3221225472 | bytes 8388608 | tf_op jit(solution)/shard_map/query_pass/pallas_call | solution.py:362
  216.4 0.8 broadcast_in_dim.71
  217.2 10.2 %all_to_all.25 = f32[4,8,2,4,128]{4,3,2,1,0:T(4,128)} all-to-all(f32[4,8,2,4,128]{4,3,2,1,0:T(4,128)S(1)} %broadcast_in_dim.71), channel_id=1, replica_groups=mesh['blk'=4,'z'=4,'x'=2] {'z'}, dimensions={0} | all-to-all | bytes 262144 | tf_op jit(solution)/shard_map/all_to_all | solution.py:375
  227.4 4.4 %all-to-all-start.2 = ((bf16[8,2,128,512]{3,2,1,0:T(8,128)(2,1)}), bf16[8,2,128,512]{3,2,1,0:T(8,128)(2,1)}, u32[]{:S(2)}, u32[]{:S(2)}) async-start(bf16[8,2,128,512]{3,2,1,0:T(8,128)(2,1)} %get-tuple-element.137), calls=%async_computation.2 | async-start | bytes 4194304 | tf_op jit(solution)/shard_map/all_to_all | solution.py:304
  231.9 1.7 slice_bitcast_fusion
  233.6 3.1 collective-permute-start.5
  236.7 1.3 collective-permute-start.6
  238.0 21.7 %collective-permute-done.5.below = bf16[4,2,128,512]{3,2,1,0:T(8,128)(2,1)S(1)} collective-permute-done((bf16[4,2,128,512]{3,2,1,0:T(8,128)(2,1)S(1)}, bf16[4,2,128,512]{3,2,1,0:T(8,128)(2,1)S(1)}, u32[]{:S(2)}, u32[]{:S(2)}) %collective-permute-start.5) | collective-permute-done | bytes 1048608 | tf_op jit(solution)/shard_map/ppermute | solution.py:319
  259.7 4.3 %collective-permute-done.6.above = bf16[4,2,128,512]{3,2,1,0:T(8,128)(2,1)} collective-permute-done((bf16[4,2,128,512]{3,2,1,0:T(8,128)(2,1)S(1)}, bf16[4,2,128,512]{3,2,1,0:T(8,128)(2,1)}, u32[]{:S(2)}, u32[]{:S(2)}) %collective-permute-start.6) | collective-permute-done | bytes 1048608 | tf_op jit(solution)/shard_map/ppermute | solution.py:320
  264.0 13.5 %key_pass.1 = bf16[8,2,128,512]{3,2,1,0:T(8,128)(2,1)} custom-call(s32[8,6]{1,0:T(8,128)} %add_select_fusion.3.slot_ref, s32[8,6]{1,0:T(8,128)} %get-tuple-element.200.valid_ref, s32[8,6]{1,0:T(8,128)} %get-tuple-element.198.place_ref, s32[8]{0:T(128)} %reduce_sum.165.cross_ref, s32[1]{0:T(128)} %bitcast.7.count_ref, ...), custom_call_target="tpu_custom_call" | custom-call | flops 3221225472 | bytes 8388608 | tf_op jit(solution)/shard_map/key_pass/pallas_call | solution.py:377
  277.5 3.8 %all-to-all-start.4 = ((bf16[8,2,128,512]{3,2,1,0:T(8,128)(2,1)}), bf16[8,2,128,512]{3,2,1,0:T(8,128)(2,1)S(1)}, u32[]{:S(2)}, u32[]{:S(2)}) async-start(bf16[8,2,128,512]{3,2,1,0:T(8,128)(2,1)} %key_pass.1), calls=%async_computation.4 | async-start | bytes 4194304 | tf_op jit(solution)/shard_map/all_to_all | solution.py:304
  281.3 2.6 unpack.2
  283.9 23.5 %all-to-all-done.4.in_ref = bf16[8,2,128,512]{3,2,1,0:T(8,128)(2,1)S(1)} async-done(((bf16[8,2,128,512]{3,2,1,0:T(8,128)(2,1)}), bf16[8,2,128,512]{3,2,1,0:T(8,128)(2,1)S(1)}, u32[]{:S(2)}, u32[]{:S(2)}) %all-to-all-start.4) | async-done | bytes 2097184 | tf_op jit(solution)/shard_map/all_to_all | solution.py:304
  307.3 1.3 copy-done
  308.7 2.6 unpack.3
  (64 shorter events, 5.6 us)
Async XLA Ops:
  0.6 8.0 %copy-start.2 = (s32[32,32]{1,0:T(8,128)S(1)}, s32[32,32]{1,0:T(8,128)}, u32[]{:S(2)}) copy-start(s32[32,32]{1,0:T(8,128)} %param.15) | copy-start | bytes 12292
  3.3 31.2 %all-to-all-start.1 = ((bf16[8,2,128,512]{3,2,1,0:T(8,128)(2,1)}), bf16[8,2,128,512]{3,2,1,0:T(8,128)(2,1)S(1)}, u32[]{:S(2)}, u32[]{:S(2)}) async-start(bf16[8,2,128,512]{3,2,1,0:T(8,128)(2,1)} %pack.3), calls=%async_computation.1 | async-start | bytes 4194304 | tf_op jit(solution)/shard_map/all_to_all | solution.py:304
  34.6 30.4 %all-to-all-start = ((bf16[8,2,128,512]{3,2,1,0:T(8,128)(2,1)}), bf16[8,2,128,512]{3,2,1,0:T(8,128)(2,1)}, u32[]{:S(2)}, u32[]{:S(2)}) async-start(bf16[8,2,128,512]{3,2,1,0:T(8,128)(2,1)} %pack.2), calls=%async_computation | async-start | bytes 4194304 | tf_op jit(solution)/shard_map/all_to_all | solution.py:304
  42.1 149.9 %collective-permute-start.3 = (bf16[4,2,128,512]{3,2,1,0:T(8,128)(2,1)}, bf16[4,2,128,512]{3,2,1,0:T(8,128)(2,1)}, u32[]{:S(2)}, u32[]{:S(2)}) collective-permute-start(bf16[4,2,128,512]{3,2,1,0:T(8,128)(2,1)} %get-tuple-element.220), channel_id=1, source_target_pairs={{0,2},{2,4},{4,6},{1,3},{3,5},{5,7},{8,10},{10,12},{12,14},{9,11},... | collective-permute-start | bytes 3145736 | tf_op jit(solution)/shard_map/ppermute | solution.py:319
  46.6 145.4 %collective-permute-start.4 = (bf16[4,2,128,512]{3,2,1,0:T(8,128)(2,1)}, bf16[4,2,128,512]{3,2,1,0:T(8,128)(2,1)}, u32[]{:S(2)}, u32[]{:S(2)}) collective-permute-start(bf16[4,2,128,512]{3,2,1,0:T(8,128)(2,1)} %get-tuple-element.219), channel_id=1, source_target_pairs={{2,0},{4,2},{6,4},{3,1},{5,3},{7,5},{10,8},{12,10},{14,12},{11,9},... | collective-permute-start | bytes 3145736 | tf_op jit(solution)/shard_map/ppermute | solution.py:320
  71.1 25.8 %collective-permute-start.1 = (bf16[2,2,128,512]{3,2,1,0:T(8,128)(2,1)S(1)}, bf16[2,2,128,512]{3,2,1,0:T(8,128)(2,1)S(1)}, u32[]{:S(2)}, u32[]{:S(2)}) collective-permute-start(bf16[2,2,128,512]{3,2,1,0:T(8,128)(2,1)S(1)} %pad_maximum_fusion.7), channel_id=1, source_target_pairs={{0,4},{2,6},{4,0},{6,2},{1,5},{3,7},{5,1},{7,3},{8,12},{10,14},{12... | collective-permute-start | bytes 1572872 | tf_op jit(solution)/shard_map/while/body/ppermute | solution.py:341
  103.3 25.0 %collective-permute-start.1 = (bf16[2,2,128,512]{3,2,1,0:T(8,128)(2,1)S(1)}, bf16[2,2,128,512]{3,2,1,0:T(8,128)(2,1)S(1)}, u32[]{:S(2)}, u32[]{:S(2)}) collective-permute-start(bf16[2,2,128,512]{3,2,1,0:T(8,128)(2,1)S(1)} %pad_maximum_fusion.7), channel_id=1, source_target_pairs={{0,4},{2,6},{4,0},{6,2},{1,5},{3,7},{5,1},{7,3},{8,12},{10,14},{12... | collective-permute-start | bytes 1572872 | tf_op jit(solution)/shard_map/while/body/ppermute | solution.py:341
  134.7 24.2 %collective-permute-start.1 = (bf16[2,2,128,512]{3,2,1,0:T(8,128)(2,1)S(1)}, bf16[2,2,128,512]{3,2,1,0:T(8,128)(2,1)S(1)}, u32[]{:S(2)}, u32[]{:S(2)}) collective-permute-start(bf16[2,2,128,512]{3,2,1,0:T(8,128)(2,1)S(1)} %pad_maximum_fusion.7), channel_id=1, source_target_pairs={{0,4},{2,6},{4,0},{6,2},{1,5},{3,7},{5,1},{7,3},{8,12},{10,14},{12... | collective-permute-start | bytes 1572872 | tf_op jit(solution)/shard_map/while/body/ppermute | solution.py:341
  165.3 24.6 %collective-permute-start.1 = (bf16[2,2,128,512]{3,2,1,0:T(8,128)(2,1)S(1)}, bf16[2,2,128,512]{3,2,1,0:T(8,128)(2,1)S(1)}, u32[]{:S(2)}, u32[]{:S(2)}) collective-permute-start(bf16[2,2,128,512]{3,2,1,0:T(8,128)(2,1)S(1)} %pad_maximum_fusion.7), channel_id=1, source_target_pairs={{0,4},{2,6},{4,0},{6,2},{1,5},{3,7},{5,1},{7,3},{8,12},{10,14},{12... | collective-permute-start | bytes 1572872 | tf_op jit(solution)/shard_map/while/body/ppermute | solution.py:341
  227.4 50.0 %all-to-all-start.2 = ((bf16[8,2,128,512]{3,2,1,0:T(8,128)(2,1)}), bf16[8,2,128,512]{3,2,1,0:T(8,128)(2,1)}, u32[]{:S(2)}, u32[]{:S(2)}) async-start(bf16[8,2,128,512]{3,2,1,0:T(8,128)(2,1)} %get-tuple-element.137), calls=%async_computation.2 | async-start | bytes 4194304 | tf_op jit(solution)/shard_map/all_to_all | solution.py:304
  233.6 26.1 %collective-permute-start.5 = (bf16[4,2,128,512]{3,2,1,0:T(8,128)(2,1)S(1)}, bf16[4,2,128,512]{3,2,1,0:T(8,128)(2,1)S(1)}, u32[]{:S(2)}, u32[]{:S(2)}) collective-permute-start(bf16[4,2,128,512]{3,2,1,0:T(8,128)(2,1)S(1)} %get-tuple-element.218), channel_id=1, source_target_pairs={{0,2},{2,4},{4,6},{1,3},{3,5},{5,7},{8,10},{10,12},{12,14},{9,11},... | collective-permute-start | bytes 3145736 | tf_op jit(solution)/shard_map/ppermute | solution.py:319
  236.7 27.3 %collective-permute-start.6 = (bf16[4,2,128,512]{3,2,1,0:T(8,128)(2,1)S(1)}, bf16[4,2,128,512]{3,2,1,0:T(8,128)(2,1)}, u32[]{:S(2)}, u32[]{:S(2)}) collective-permute-start(bf16[4,2,128,512]{3,2,1,0:T(8,128)(2,1)S(1)} %get-tuple-element.217), channel_id=1, source_target_pairs={{2,0},{4,2},{6,4},{3,1},{5,3},{7,5},{10,8},{12,10},{14,12},{11,9},... | collective-permute-start | bytes 3145736 | tf_op jit(solution)/shard_map/ppermute | solution.py:320
  259.7 4.3 %copy-start.1 = (bf16[4,2,128,512]{3,2,1,0:T(8,128)(2,1)}, bf16[4,2,128,512]{3,2,1,0:T(8,128)(2,1)S(1)}, u32[]{:S(2)}) copy-start(bf16[4,2,128,512]{3,2,1,0:T(8,128)(2,1)S(1)} %collective-permute-done.5.below) | copy-start | bytes 3145732
  277.5 29.8 %all-to-all-start.4 = ((bf16[8,2,128,512]{3,2,1,0:T(8,128)(2,1)}), bf16[8,2,128,512]{3,2,1,0:T(8,128)(2,1)S(1)}, u32[]{:S(2)}, u32[]{:S(2)}) async-start(bf16[8,2,128,512]{3,2,1,0:T(8,128)(2,1)} %key_pass.1), calls=%async_computation.4 | async-start | bytes 4194304 | tf_op jit(solution)/shard_map/all_to_all | solution.py:304
  307.3 1.4 copy-start
where the time goes:
time: 312 us; the launch traced here: 311 us
  waiting for transfers between devices  178 us (57%)
  Pallas kernels  48.4 us (16%)
  starting transfers between devices  30.8 us (10%)
  loops' own time  17.4 us (6%)
  local copies, waits for them, and re-layouts  17.1 us (5%)
  blocking collectives  10.2 us (3%)
  other arithmetic  6.36 us (2%)
    ppermute x4, waiting for transfers between devices, one_round(): got = lax.ppermute(sent, 'z', swap)  96.7 us
    all_to_all x4, waiting for transfers between devices, exchange(): lax.all_to_all(pair, ('blk', 'x'), split_axis=0, concat_axis=0, tiled=True)  55.5 us
    pallas_call x1, Pallas kernels, shards(): pl.pallas_call(functools.partial(query_kernel, width, heads), out_shape=(...  24.4 us
    ppermute x2, waiting for transfers between devices, neighbours(): below = lax.ppermute(edges[:, SUB - 1], 'z', upward)  21.7 us
    all_to_all x4, starting transfers between devices, exchange(): lax.all_to_all(pair, ('blk', 'x'), split_axis=0, concat_axis=0, tiled=True)  17.8 us
    another operation x3, loops' own time, shards(): extra = lax.fori_loop(0, rounds[d - 1], one_round, extra)  17.4 us
    pallas_call x1, Pallas kernels, shards(): pl.pallas_call(functools.partial(key_kernel, width, heads), out_shape=jax...  13.5 us
    all_to_all x1, blocking collectives, shards(): lax.all_to_all(spread, 'z', split_axis=0, concat_axis=0, tiled=True)  10.2 us
  transfers between devices with their start and end apart: 12, of which 9 were waited for; matrix products, arithmetic and copies ran while one was open for 7% of the time, Pallas kernels for 6%

commit v1 on v0

v1 whole, which is shorter than its diff:
```python
import functools
import math
import jax
import jax.numpy as jnp
from jax import lax
from jax.experimental import pallas as pl
from jax.experimental.pallas import tpu as pltpu
from jax.sharding import Mesh, PartitionSpec as P

HEAD_DIM = 128
BLOCK = 128
SUB = 2
NEG = float("-inf")
POS = float("inf")
BF16 = jnp.bfloat16
F32 = jnp.float32
SCALE = HEAD_DIM ** (-0.5)
SCALE2 = SCALE * math.log2(math.e)
OWN = 3


def head_of(h):
    return slice(h * HEAD_DIM, (h + 1) * HEAD_DIM)


def dot_nt(a, b):
    return lax.dot_general(a, b, (((1,), (1,)), ((), ())), preferred_element_type=F32)


def dot_nn(a, b):
    return lax.dot_general(a, b, (((1,), (0,)), ((), ())), preferred_element_type=F32)


def pack_kernel(a_ref, b_ref, out_ref, sem):
    groups, _, _, columns = out_ref.shape
    copies = [
        pltpu.make_async_copy(
            source.at[:, c * columns : (c + 1) * columns], out_ref.at[c, n], sem.at[c, n]
        )
        for c in range(groups)
        for n, source in enumerate((a_ref, b_ref))
    ]
    for copy in copies:
        copy.start()
    for copy in copies:
        copy.wait()


def unpack_kernel(in_ref, a_ref, b_ref, sem):
    groups, _, _, columns = in_ref.shape
    copies = [
        pltpu.make_async_copy(
            in_ref.at[c, n], target.at[:, c * columns : (c + 1) * columns], sem.at[c, n]
        )
        for c in range(groups)
        for n, target in enumerate((a_ref, b_ref))
    ]
    for copy in copies:
        copy.start()
    for copy in copies:
        copy.wait()


def pack(a, b, groups):
    rows, columns = a.shape
    anywhere = pl.BlockSpec(memory_space=pl.ANY)
    return pl.pallas_call(
        pack_kernel,
        out_shape=jax.ShapeDtypeStruct((groups, 2, rows, columns // groups), a.dtype),
        in_specs=[anywhere] * 2,
        out_specs=pl.BlockSpec(memory_space=pltpu.VMEM),
        scratch_shapes=[pltpu.SemaphoreType.DMA((groups, 2))],
        name="pack",
    )(a, b)


def unpack(pair):
    groups, _, rows, columns = pair.shape
    anywhere = pl.BlockSpec(memory_space=pl.ANY)
    flat = jax.ShapeDtypeStruct((rows, groups * columns), pair.dtype)
    return pl.pallas_call(
        unpack_kernel,
        out_shape=(flat, flat),
        in_specs=[pl.BlockSpec(memory_space=pltpu.VMEM)],
        out_specs=(anywhere, anywhere),
        scratch_shapes=[pltpu.SemaphoreType.DMA((groups, 2))],
        name="unpack",
    )(pair)


def fill_pool(count, parts, pool, extra, sem, extra_sem):
    copies = []
    start = 0
    for m, source in enumerate(parts):
        size = source.shape[0]
        copies.append(pltpu.make_async_copy(source, pool.at[pl.ds(start, size)], sem.at[m]))
        start += size
    for copy in copies:
        copy.start()

    def move(slot):
        return pltpu.make_async_copy(extra.at[slot], pool.at[start + slot], extra_sem.at[slot])

    lax.fori_loop(0, count, lambda slot, _: (move(slot).start(), 0)[1], 0)
    for copy in copies:
        copy.wait()
    lax.fori_loop(0, count, lambda slot, _: (move(slot).wait(), 0)[1], 0)


def by_width(cross, width, body):
    top = min(OWN, width - OWN)
    for n in range(top):

        @pl.when(cross == n)
        def _(n=n):
            body(OWN + n)

    @pl.when(cross >= top)
    def _():
        body(width)


def unsure(t):
    return t == OWN - 1 or t >= 2 * OWN


def query_kernel(
    width, heads, slot_ref, valid_ref, cross_ref, count_ref, qg_ref, kv_local, below, above, extra,
    out_ref, stat_ref, pool, sem, extra_sem,
):
    fill_pool(count_ref[0], (kv_local, below, above), pool, extra, sem, extra_sem)
    lane = lax.broadcasted_iota(jnp.int32, (BLOCK, BLOCK), 1)

    def block(i, _):
        def body(count):
            slots = [slot_ref[i, t] for t in range(count)]
            bias = jnp.concatenate(
                [
                    jnp.full((1, BLOCK), jnp.where(valid_ref[i, t] > 0, 0.0, NEG), F32)
                    if unsure(t)
                    else jnp.zeros((1, BLOCK), F32)
                    for t in range(count)
                ],
                axis=1,
            )
            every = range(heads)
            keys = [jnp.concatenate([pool[s, 0, :, head_of(h)] for s in slots], axis=0) for h in every]
            values = [jnp.concatenate([pool[s, 1, :, head_of(h)] for s in slots], axis=0) for h in every]
            upstream = [qg_ref[i, 1, :, head_of(h)] for h in every]
            scores = [dot_nt(qg_ref[i, 0, :, head_of(h)], keys[h]) * SCALE2 + bias for h in every]
            dprobs = [dot_nt(upstream[h], values[h]) for h in every]
            peaks = [jnp.max(scores[h], axis=1, keepdims=True) for h in every]
            probs = [jnp.exp2(scores[h] - peaks[h]) for h in every]
            totals = [jnp.sum(probs[h], axis=1, keepdims=True) for h in every]
            scales = [1.0 / totals[h] for h in every]
            outs = [dot_nn(probs[h].astype(BF16), values[h]) * scales[h] for h in every]
            deltas = [
                jnp.sum(upstream[h].astype(F32) * outs[h], axis=1, keepdims=True) for h in every
            ]
            dscores = [(probs[h] * (dprobs[h] - deltas[h])).astype(BF16) for h in every]
            grads = [dot_nn(dscores[h], keys[h]) * (scales[h] * SCALE) for h in every]
            stats = jnp.zeros((BLOCK, BLOCK), F32)
            for h in every:
                stats = jnp.where(lane == h, peaks[h] + jnp.log2(totals[h]), stats)
                stats = jnp.where(lane == heads + h, deltas[h], stats)
            for h in every:
                out_ref[i, 0, :, head_of(h)] = outs[h].astype(BF16)
                out_ref[i, 1, :, head_of(h)] = grads[h].astype(BF16)
            stat_ref[i] = stats.T[: 2 * heads]

        by_width(cross_ref[i], width, body)
        return 0

    lax.fori_loop(0, qg_ref.shape[0], block, 0)


def key_kernel(
    width, heads, slot_ref, valid_ref, place_ref, cross_ref, count_ref, kv_ref, stat_ref, qg_local,
    below, above, extra, out_ref, pool, sem, extra_sem,
):
    fill_pool(count_ref[0], (qg_local, below, above), pool, extra, sem, extra_sem)

    def block(j, _):
        def body(count):
            slots = [slot_ref[j, t] for t in range(count)]
            places = [place_ref[j, t] for t in range(count)]

            def log_tile(t, h):
                row = stat_ref[places[t], pl.ds(h, 1), :]
                return jnp.where(valid_ref[j, t] > 0, row, POS) if unsure(t) else row

            every = range(heads)
            queries = [jnp.concatenate([pool[s, 0, :, head_of(h)] for s in slots], axis=0) for h in every]
            upstream = [jnp.concatenate([pool[s, 1, :, head_of(h)] for s in slots], axis=0) for h in every]
            logs = [jnp.concatenate([log_tile(t, h) for t in range(count)], axis=1) for h in every]
            deltas = [
                jnp.concatenate([stat_ref[p, pl.ds(heads + h, 1), :] for p in places], axis=1)
                for h in every
            ]
            scores = [dot_nt(kv_ref[j, 0, :, head_of(h)], queries[h]) for h in every]
            dprobs = [dot_nt(kv_ref[j, 1, :, head_of(h)], upstream[h]) for h in every]
            probs = [jnp.exp2(scores[h] * SCALE2 - logs[h]) for h in every]
            dscores = [(probs[h] * (dprobs[h] - deltas[h])).astype(BF16) for h in every]
            grad_v = [dot_nn(probs[h].astype(BF16), upstream[h]) for h in every]
            grad_k = [dot_nn(dscores[h], queries[h]) * SCALE for h in every]
            for h in every:
                out_ref[j, 1, :, head_of(h)] = grad_v[h].astype(BF16)
                out_ref[j, 0, :, head_of(h)] = grad_k[h].astype(BF16)

        by_width(cross_ref[j], width, body)
        return 0

    lax.fori_loop(0, kv_ref.shape[0], block, 0)


def patterns_of(steps):
    groups, index = [], {}
    for d in range(1, steps):
        top = 1 << (d.bit_length() - 1)
        for low in range(top):
            pairs = [a for a in range(steps) if not a & top and a % top == low]
            for a in pairs:
                index[a, a ^ d] = index[a ^ d, a] = len(groups)
            groups.append([(a, a ^ d) for a in pairs] + [(a ^ d, a) for a in pairs])
    return groups, index


def tables(block_mask, spans, span_len, steps, groups):
    z = lax.axis_index("z")
    local = spans * SUB
    most = (spans * (spans - 1) + len(groups)) // 2
    capacity = 2 * most
    iota = functools.partial(lax.broadcasted_iota, jnp.int32)
    as_int = lambda flags: flags.astype(jnp.int32)
    cube = block_mask.reshape(spans, span_len, spans, span_len)
    partner = jnp.sum(cube * (iota(cube.shape, 3) + 1), axis=3) - 1
    shape = partner.shape
    mine, spot, other = iota(shape, 0), iota(shape, 1), iota(shape, 2)
    linked = (partner >= 0) & (mine != other)
    here, there = spot // SUB, partner // SUB
    hop = jnp.where(linked, here ^ there, 0)
    top = sum(as_int(hop >= (1 << n)) << n for n in range(steps.bit_length()))
    top = (top + 1) // 2
    low = jnp.minimum(here, there) & (jnp.maximum(top, 1) - 1)
    group = jnp.where(hop > 0, base_of(hop, top) + low, -1)
    per_place = group.reshape(spans, steps, SUB, spans)
    numbers = iota((len(groups), spans, steps, SUB, spans), 0)
    rounds = (jnp.max(jnp.sum(as_int(per_place[None] == numbers), axis=(1, 3, 4)), axis=1) + 1) // 2
    number = iota((len(groups), len(groups)), 0)
    ends = jnp.sum(jnp.where(number <= iota(number.shape, 1), rounds[:, None], 0), axis=0)
    starts = ends - rounds
    total = jnp.sum(rounds)
    at = iota((most, len(groups)), 0)
    plan = jnp.minimum(jnp.sum(as_int(at >= ends[None]), axis=1), len(groups) - 1)
    key = jnp.where(
        mine < other,
        (mine * span_len + spot) * spans + other,
        (other * span_len + partner) * spans + mine,
    )

    def at_place(table):
        return lax.dynamic_slice_in_dim(table, z * SUB, SUB, 1).reshape(local, spans)

    partner_l, linked_l, group_l, key_l = [at_place(t) for t in (partner, linked, group, key)]
    other_l = iota((local, spans), 1)
    block_l = iota((local, spans), 0)
    order = (group_l * (spans * span_len * spans) + key_l).reshape(-1)
    flat = group_l.reshape(-1)
    crossing = flat >= 0
    same = crossing[None, :] & (flat[None, :] == flat[:, None])
    rank = jnp.sum(as_int(same & (order[None, :] < order[:, None])), axis=1)
    first = jnp.sum(
        jnp.where(flat[:, None] == iota((local * spans, len(groups)), 1), starts[None], 0), axis=1
    )
    extra_slot = 2 * first + rank
    hits = crossing[:, None] & (extra_slot[:, None] == iota((local * spans, capacity), 1))
    send_block = jnp.sum(as_int(hits) * block_l.reshape(-1)[:, None], axis=0).reshape(most, 2)
    plan = (plan * local + send_block[:, 0]) * local + send_block[:, 1]
    cross_slot = jnp.where(
        group_l >= 0,
        local + 2 * spans + extra_slot.reshape(local, spans),
        other_l * SUB + partner_l % SUB,
    )
    cross_place = (z ^ (partner_l // SUB)) * local + other_l * SUB + partner_l % SUB
    own = block_l[:, :1]
    span_l, x_l = own // SUB, own % SUB
    pair = own + 1 - 2 * x_l
    near_slot = jnp.where(x_l == 0, local + span_l, local + spans + span_l)
    near_ok = jnp.where(x_l == 0, z > 0, z < steps - 1)
    near_place = jnp.where(x_l == 0, (z ^ (z - 1)) * local + own + 1, (z ^ (z + 1)) * local + own - 1)
    before = iota((local, spans, spans), 2) < iota((local, spans, spans), 1)
    position = jnp.sum(as_int(linked_l[:, None, :] & before), axis=2)
    chosen = linked_l[:, None, :] & (position[:, None, :] == iota((local, spans - 1, spans), 1))

    def pick(table):
        return jnp.sum(jnp.where(chosen, table[:, None, :], 0), axis=2)

    sure = jnp.ones_like(own)
    ok = jnp.concatenate([sure, sure, as_int(near_ok), pick(as_int(linked_l))], axis=1)
    slot = jnp.concatenate([own, pair, near_slot, pick(cross_slot)], axis=1)
    place = jnp.concatenate([own, pair, near_place, pick(cross_place)], axis=1)
    slot = jnp.where(ok > 0, slot, own)
    place = jnp.where(ok > 0, place, own)
    cross = jnp.sum(as_int(linked_l), axis=1)
    return slot, ok, place, cross, total, plan, capacity


def base_of(hop, top):
    smaller = (top * top - 1) // 3
    return smaller + (hop - top) * top


def shards(query_tokens, key_tokens, value_tokens, cotangent, block_mask):
    spans = lax.axis_size("blk")
    steps = lax.axis_size("z")
    span_len = steps * SUB
    local = spans * SUB
    groups, _ = patterns_of(steps)

    def exchange(pair):
        return lax.all_to_all(pair, ("blk", "x"), split_axis=0, concat_axis=0, tiled=True)

    kv = exchange(pack(key_tokens, value_tokens, local))
    qg = exchange(pack(query_tokens, cotangent, local))
    columns = kv.shape[3]
    heads = columns // HEAD_DIM
    slot, ok, place, cross, total, plan, capacity = tables(
        block_mask, spans, span_len, steps, groups
    )
    width = slot.shape[1]
    upward = [(n, n + 1) for n in range(steps - 1)]
    downward = [(n + 1, n) for n in range(steps - 1)]

    def neighbours(pair):
        edges = pair.reshape(spans, SUB, 2, BLOCK, columns)
        below = lax.ppermute(edges[:, SUB - 1], "z", upward)
        above = lax.ppermute(edges[:, 0], "z", downward)
        return below, above

    kv_below, kv_above = neighbours(kv)
    qg_below, qg_above = neighbours(qg)

    def crossing(pair):
        buffer = pl.pallas_call(
            lambda out_ref: None,
            out_shape=jax.ShapeDtypeStruct((capacity, 2, BLOCK, columns), BF16),
            out_specs=pl.BlockSpec(memory_space=pl.ANY),
            name="extra_blocks",
        )()
        swaps = [functools.partial(lax.ppermute, axis_name="z", perm=g) for g in groups]

        def one_round(r, held):
            code = plan[r]
            first, second = code // local % local, code % local
            sent = jnp.concatenate(
                [lax.dynamic_slice_in_dim(pair, n, 1, 0) for n in (first, second)]
            )
            got = lax.switch(code // (local * local), swaps, sent)
            return lax.dynamic_update_slice_in_dim(held, got, 2 * r, 0)

        return lax.fori_loop(0, total, one_round, buffer)

    kv_extra = crossing(kv)
    qg_extra = crossing(qg)
    count = 2 * total.reshape(1)

    smem = pl.BlockSpec(memory_space=pltpu.SMEM)
    vmem = pl.BlockSpec(memory_space=pltpu.VMEM)
    anywhere = pl.BlockSpec(memory_space=pl.ANY)
    scratch = [
        pltpu.VMEM((local + 2 * spans + capacity, 2, BLOCK, columns), BF16),
        pltpu.SemaphoreType.DMA((3,)),
        pltpu.SemaphoreType.DMA((capacity,)),
    ]
    cost = pl.CostEstimate(
        flops=2 * 4 * local * heads * width * BLOCK * BLOCK * HEAD_DIM,
        bytes_accessed=16 * local * BLOCK * columns,
        transcendentals=local * heads * width * BLOCK * BLOCK,
    )
    out_pair, stats = pl.pallas_call(
        functools.partial(query_kernel, width, heads),
        out_shape=(
            jax.ShapeDtypeStruct(qg.shape, BF16),
            jax.ShapeDtypeStruct((local, 2 * heads, BLOCK), F32),
        ),
        in_specs=[smem] * 4 + [vmem] + [anywhere] * 4,
        out_specs=(vmem, vmem),
        scratch_shapes=scratch,
        cost_estimate=cost,
        name="query_pass",
    )(slot, ok, cross, count, qg, kv, kv_below, kv_above, kv_extra)
    far = [lax.ppermute(stats, "z", [(n, n ^ d) for n in range(steps)]) for d in range(1, steps)]
    all_stats = jnp.concatenate([stats] + far)
    grad_pair = pl.pallas_call(
        functools.partial(key_kernel, width, heads),
        out_shape=jax.ShapeDtypeStruct(kv.shape, BF16),
        in_specs=[smem] * 5 + [vmem, vmem] + [anywhere] * 4,
        out_specs=vmem,
        scratch_shapes=scratch,
        cost_estimate=cost,
        name="key_pass",
    )(slot, ok, place, cross, count, kv, all_stats, qg, qg_below, qg_above, qg_extra)
    out_back = exchange(out_pair)
    grad_back = exchange(grad_pair)
    attended, grad_query = unpack(out_back)
    grad_key, grad_value = unpack(grad_back)
    return attended, grad_query, grad_key, grad_value


def solution(mesh):
    spans, ulysses = mesh.shape["blk"], mesh.shape["ulysses"]
    split = Mesh(mesh.devices.reshape(spans, ulysses // SUB, SUB), ("blk", "z", "x"))
    tokens = P(("blk", "z", "x"), None)
    return jax.shard_map(
        shards,
        mesh=split,
        in_specs=(tokens, tokens, tokens, tokens, P()),
        out_specs=(tokens, tokens, tokens, tokens),
        check_vma=False,
    )
```

time: 312 us -> 255 us (0.82)
  waiting for transfers between devices: 178 us -> 61.2 us
  starting transfers between devices: 30.8 us -> 114 us
  Pallas kernels: 48.4 us -> 36.3 us
  blocking collectives: 10.2 us -> 0 us
  local copies, waits for them, and re-layouts: 17.1 us -> 21 us
    ppermute x4 -> x7, waiting for transfers between devices: 96.7 us -> 4.35 us  [the longest x3 4.34 us: shards(): lax.ppermute(stats, 'z', [(n, n ^ d) for n in range(steps)])]
    ppermute x4 -> x7, starting transfers between devices: 2.87 us -> 84.9 us  [the longest x3 79 us: shards(): lax.ppermute(stats, 'z', [(n, n ^ d) for n in range(steps)])]
    ppermute x2, waiting for transfers between devices: 21.7 us -> 0.01 us  [neighbours(): below = lax.ppermute(edges[:, SUB - 1], 'z', upward)]
    pallas_call x1, Pallas kernels: 24.4 us -> 12.9 us  [shards(): pl.pallas_call(functools.partial(query_kernel, width, heads), out_shape=(...]
    all_to_all x1 -> x0, blocking collectives: 10.2 us -> none  [shards(): lax.all_to_all(spread, 'z', split_axis=0, concat_axis=0, tiled=True)]
    ppermute x2, waiting for transfers between devices: 4.29 us -> 0.01 us  [neighbours(): above = lax.ppermute(edges[:, 0], 'z', downward)]
    dynamic_update_slice x4, local copies, waits for them, and re-layouts: 3.37 us -> 7.47 us  [one_round(): return lax.dynamic_update_slice_in_dim(held, got, 2 * r, 0)]
    another operation x3 -> x6, loops' own time: 17.4 us -> 14.4 us  [the longest x2 14.4 us: crossing(): return lax.fori_loop(0, total, one_round, buffer)]
  transfers between devices with their start and end apart: 12 -> 15, of which waited for: 9 -> 5; matrix products, arithmetic and copies ran while one was open for 7% -> 9% of each run, Pallas kernels for 6% -> 12%
where the time goes in v1:
time: 255 us; the launch traced here: 254 us
  starting transfers between devices  114 us (45%)
  waiting for transfers between devices  61.2 us (24%)
  Pallas kernels  36.3 us (14%)
  local copies, waits for them, and re-layouts  21 us (8%)
  loops' own time  14.4 us (6%)
  other arithmetic  5.08 us (2%)
    ppermute x3, starting transfers between devices, shards(): lax.ppermute(stats, 'z', [(n, n ^ d) for n in range(steps)])  79 us
    all_to_all x4, waiting for transfers between devices, exchange(): lax.all_to_all(pair, ('blk', 'x'), split_axis=0, concat_axis=0, tiled=True)  56.8 us
    all_to_all x4, starting transfers between devices, exchange(): lax.all_to_all(pair, ('blk', 'x'), split_axis=0, concat_axis=0, tiled=True)  17.5 us
    another operation x2, loops' own time, crossing(): return lax.fori_loop(0, total, one_round, buffer)  14.4 us
    pallas_call x1, Pallas kernels, shards(): pl.pallas_call(functools.partial(query_kernel, width, heads), out_shape=(...  12.9 us
    pallas_call x1, Pallas kernels, shards(): pl.pallas_call(functools.partial(key_kernel, width, heads), out_shape=jax...  11.2 us
    ppermute x2, starting transfers between devices, neighbours(): below = lax.ppermute(edges[:, SUB - 1], 'z', upward)  8.97 us
    dynamic_update_slice x4, local copies, waits for them, and re-layouts, one_round(): return lax.dynamic_update_slice_in_dim(held, got, 2 * r, 0)  7.47 us
  transfers between devices with their start and end apart: 15, of which 5 were waited for; matrix products, arithmetic and copies ran while one was open for 9% of the time, Pallas kernels for 12%

profile of v1, /device:TPU:0, one launch (start us, length us, event | category | flops | bytes accessed | tf_op | source)
XLA Modules:
  0.0 253.7 jit_solution(14726963473244337885)
XLA Ops:
  0.6 3.1 %pack.3 = bf16[8,2,128,512]{3,2,1,0:T(8,128)(2,1)} custom-call(bf16[128,4096]{1,0:T(8,128)(2,1)} %a_ref.3, bf16[128,4096]{1,0:T(8,128)(2,1)} %b_ref.3), custom_call_target="tpu_custom_call" | custom-call | tf_op jit(solution)/shard_map/pack/pallas_call | solution.py:67
  3.8 5.2 %all-to-all-start.1 = ((bf16[8,2,128,512]{3,2,1,0:T(8,128)(2,1)}), bf16[8,2,128,512]{3,2,1,0:T(8,128)(2,1)S(1)}, u32[]{:S(2)}, u32[]{:S(2)}) async-start(bf16[8,2,128,512]{3,2,1,0:T(8,128)(2,1)} %pack.3), calls=%async_computation.1 | async-start | bytes 4194304 | tf_op jit(solution)/shard_map/all_to_all | solution.py:321
  9.1 0.7 copy-done.2
  11.4 0.6 fusion.33
  15.1 3.1 %pack.2 = bf16[8,2,128,512]{3,2,1,0:T(8,128)(2,1)} custom-call(bf16[128,4096]{1,0:T(8,128)(2,1)} %a_ref.2, bf16[128,4096]{1,0:T(8,128)(2,1)} %b_ref.2), custom_call_target="tpu_custom_call" | custom-call | tf_op jit(solution)/shard_map/pack/pallas_call | solution.py:67
  18.2 16.9 %all-to-all-done.1.kv_local.kv_ref = bf16[8,2,128,512]{3,2,1,0:T(8,128)(2,1)S(1)} async-done(((bf16[8,2,128,512]{3,2,1,0:T(8,128)(2,1)}), bf16[8,2,128,512]{3,2,1,0:T(8,128)(2,1)S(1)}, u32[]{:S(2)}, u32[]{:S(2)}) %all-to-all-start.1) | async-done | bytes 2097184 | tf_op jit(solution)/shard_map/all_to_all | solution.py:321
  35.0 4.4 %all-to-all-start = ((bf16[8,2,128,512]{3,2,1,0:T(8,128)(2,1)}), bf16[8,2,128,512]{3,2,1,0:T(8,128)(2,1)}, u32[]{:S(2)}, u32[]{:S(2)}) async-start(bf16[8,2,128,512]{3,2,1,0:T(8,128)(2,1)} %pack.2), calls=%async_computation | async-start | bytes 4194304 | tf_op jit(solution)/shard_map/all_to_all | solution.py:321
  39.9 0.7 add_select_fusion.6
  40.5 0.7 add_select_fusion.5.slot_ref
  41.2 1.5 slice_bitcast_fusion.2
  42.7 4.5 %collective-permute-start.10 = (bf16[4,2,128,512]{3,2,1,0:T(8,128)(2,1)}, bf16[4,2,128,512]{3,2,1,0:T(8,128)(2,1)}, u32[]{:S(2)}, u32[]{:S(2)}) collective-permute-start(bf16[4,2,128,512]{3,2,1,0:T(8,128)(2,1)} %get-tuple-element.294), channel_id=1, source_target_pairs={{0,2},{2,4},{4,6},{1,3},{3,5},{5,7},{8,10},{10,12},{12,14},{9,11},... | collective-permute-start | bytes 3145736 | tf_op jit(solution)/shard_map/ppermute | solution.py:336
  47.2 1.3 collective-permute-start.11
  48.4 17.0 %all-to-all-done.qg_ref.qg_local = bf16[8,2,128,512]{3,2,1,0:T(8,128)(2,1)} async-done(((bf16[8,2,128,512]{3,2,1,0:T(8,128)(2,1)}), bf16[8,2,128,512]{3,2,1,0:T(8,128)(2,1)}, u32[]{:S(2)}, u32[]{:S(2)}) %all-to-all-start) | async-done | bytes 2097184 | tf_op jit(solution)/shard_map/all_to_all | solution.py:321
  65.4 3.0 %slice_bitcast_fusion = (bf16[4,2,128,512]{3,2,1,0:T(8,128)(2,1)}, bf16[4,2,128,512]{3,2,1,0:T(8,128)(2,1)}) fusion(bf16[4,2,2,128,512]{4,3,2,1,0:T(8,128)(2,1)} %bitcast.8), kind=kLoop, calls=%fused_computation.8 | loop fusion | bytes 4194304 | tf_op jit(solution)/shard_map/squeeze | solution.py:337
  68.5 4.5 %collective-permute-start.15 = (bf16[4,2,128,512]{3,2,1,0:T(8,128)(2,1)}, bf16[4,2,128,512]{3,2,1,0:T(8,128)(2,1)}, u32[]{:S(2)}, u32[]{:S(2)}) collective-permute-start(bf16[4,2,128,512]{3,2,1,0:T(8,128)(2,1)} %get-tuple-element.292), channel_id=1, source_target_pairs={{0,2},{2,4},{4,6},{1,3},{3,5},{5,7},{8,10},{10,12},{12,14},{9,11},... | collective-permute-start | bytes 3145736 | tf_op jit(solution)/shard_map/ppermute | solution.py:336
  73.0 1.3 collective-permute-start.16
  74.3 15.5 %while.26 = (s32[]{:T(128)}, bf16[16,2,128,512]{3,2,1,0:T(8,128)(2,1)}, s32[]{:T(128)}, s32[8]{0:T(128)S(1)}, bf16[8,2,128,512]{3,2,1,0:T(8,128)(2,1)S(1)}, /*in...) while((s32[]{:T(128)}, ...), condition=%wide.region_19.20_spmd, body=%wide.region_13.19_spmd.sunk | while | flops 262200 | bytes 5243664 | solution.py:361
  74.9 0.6 dynamic_slice.115
  78.4 1.5 conditional.4
  78.4 1.5 collective-permute-start.2
  79.9 1.9 constant_dynamic-update-slice_fusion.4
  82.3 0.6 dynamic_slice.115
  85.9 1.5 conditional.4
  85.9 1.5 collective-permute-start.2
  87.4 1.9 constant_dynamic-update-slice_fusion.4
  89.8 12.9 %query_pass.1 = (bf16[8,2,128,512]{3,2,1,0:T(8,128)(2,1)}, f32[8,8,128]{2,1,0:T(8,128)}) custom-call(s32[8,6]{1,0:T(8,128)} %add_select_fusion.5.slot_ref, s32[8,6]{1,0:T(8,128)} %get-tuple-element.269.valid_ref, s32[8]{0:T(128)} %reduce_sum.128.cross_ref, s32[1]{0:T(128)} %bitcast.4.count_ref, bf16[8,2,128,512]{3,2,1,0:T(8,128)(2,1)} %all-to-all-done.qg_ref.qg_local, ...), custom_call_target="tpu_custom_call" | custom-call | flops 3221225472 | bytes 8388608 | tf_op jit(solution)/shard_map/query_pass/pallas_call | solution.py:380
  102.7 4.4 %all-to-all-start.2 = ((bf16[8,2,128,512]{3,2,1,0:T(8,128)(2,1)}), bf16[8,2,128,512]{3,2,1,0:T(8,128)(2,1)}, u32[]{:S(2)}, u32[]{:S(2)}) async-start(bf16[8,2,128,512]{3,2,1,0:T(8,128)(2,1)} %get-tuple-element.235), calls=%async_computation.2 | async-start | bytes 4194304 | tf_op jit(solution)/shard_map/all_to_all | solution.py:321
  107.1 17.2 %while.27 = (s32[]{:T(128)}, bf16[16,2,128,512]{3,2,1,0:T(8,128)(2,1)}, s32[]{:T(128)}, s32[8]{0:T(128)S(1)}, bf16[8,2,128,512]{3,2,1,0:T(8,128)(2,1)}, /*index=...) while((s32[]{:T(128)}, ...), condition=%wide.region_27.28_spmd, body=%wide.region_21.27_spmd.sunk | while | flops 262200 | bytes 5243664 | solution.py:361
  110.9 1.1 constant_dynamic-slice_fusion.11
  112.1 1.5 conditional.5
  112.1 1.5 collective-permute-start.7
  113.6 1.9 constant_dynamic-update-slice_fusion.5
  119.2 1.1 constant_dynamic-slice_fusion.11
  120.4 1.5 conditional.5
  120.4 1.5 collective-permute-start.7
  121.9 1.9 constant_dynamic-update-slice_fusion.5
  124.3 76.6 %collective-permute-start.12 = (f32[8,8,128]{2,1,0:T(8,128)S(1)}, f32[8,8,128]{2,1,0:T(8,128)S(1)}, u32[]{:S(2)}, u32[]{:S(2)}) collective-permute-start(f32[8,8,128]{2,1,0:T(8,128)S(1)} %copy-done.1), channel_id=1, source_target_pairs={{0,2},{2,0},{4,6},{6,4},{1,3},{3,1},{5,7},{7,5},{8,10},{10,8},{12,... | collective-permute-start | bytes 98312 | tf_op jit(solution)/shard_map/ppermute | solution.py:392
  200.9 1.1 collective-permute-start.13
  202.0 1.4 collective-permute-start.14
  203.3 2.4 collective-permute-done.13
  205.7 2.0 collective-permute-done.14
  207.7 0.7 pad_maximum_fusion.2.stat_ref
  208.4 11.2 %key_pass.1 = bf16[8,2,128,512]{3,2,1,0:T(8,128)(2,1)} custom-call(s32[8,6]{1,0:T(8,128)} %add_select_fusion.5.slot_ref, s32[8,6]{1,0:T(8,128)} %get-tuple-element.269.valid_ref, s32[8,6]{1,0:T(8,128)} %get-tuple-element.267.place_ref, s32[8]{0:T(128)} %reduce_sum.128.cross_ref, s32[1]{0:T(128)} %bitcast.4.count_ref, ...), custom_call_target="tpu_custom_call" | custom-call | flops 3221225472 | bytes 8388608 | tf_op jit(solution)/shard_map/key_pass/pallas_call | solution.py:394
  219.5 3.6 %all-to-all-start.3 = ((bf16[8,2,128,512]{3,2,1,0:T(8,128)(2,1)}), bf16[8,2,128,512]{3,2,1,0:T(8,128)(2,1)S(1)}, u32[]{:S(2)}, u32[]{:S(2)}) async-start(bf16[8,2,128,512]{3,2,1,0:T(8,128)(2,1)} %key_pass.1), calls=%async_computation.3 | async-start | bytes 4194304 | tf_op jit(solution)/shard_map/all_to_all | solution.py:321
  223.1 3.0 %unpack.2 = (bf16[128,4096]{1,0:T(8,128)(2,1)}, bf16[128,4096]{1,0:T(8,128)(2,1)}) custom-call(bf16[8,2,128,512]{3,2,1,0:T(8,128)(2,1)} %all-to-all-done.2.in_ref), custom_call_target="tpu_custom_call" | custom-call | tf_op jit(solution)/shard_map/unpack/pallas_call | solution.py:81
  226.2 23.0 %all-to-all-done.3.in_ref = bf16[8,2,128,512]{3,2,1,0:T(8,128)(2,1)S(1)} async-done(((bf16[8,2,128,512]{3,2,1,0:T(8,128)(2,1)}), bf16[8,2,128,512]{3,2,1,0:T(8,128)(2,1)S(1)}, u32[]{:S(2)}, u32[]{:S(2)}) %all-to-all-start.3) | async-done | bytes 2097184 | tf_op jit(solution)/shard_map/all_to_all | solution.py:321
  249.2 1.3 copy-done
  250.5 3.0 %unpack.3 = (bf16[128,4096]{1,0:T(8,128)(2,1)}, bf16[128,4096]{1,0:T(8,128)(2,1)}) custom-call(bf16[8,2,128,512]{3,2,1,0:T(8,128)(2,1)} %copy-done), custom_call_target="tpu_custom_call" | custom-call | tf_op jit(solution)/shard_map/unpack/pallas_call | solution.py:81
  (83 shorter events, 6.0 us)
Async XLA Ops:
  3.8 31.2 %all-to-all-start.1 = ((bf16[8,2,128,512]{3,2,1,0:T(8,128)(2,1)}), bf16[8,2,128,512]{3,2,1,0:T(8,128)(2,1)S(1)}, u32[]{:S(2)}, u32[]{:S(2)}) async-start(bf16[8,2,128,512]{3,2,1,0:T(8,128)(2,1)} %pack.3), calls=%async_computation.1 | async-start | bytes 4194304 | tf_op jit(solution)/shard_map/all_to_all | solution.py:321
  9.1 0.7 copy-start.2
  35.0 30.4 %all-to-all-start = ((bf16[8,2,128,512]{3,2,1,0:T(8,128)(2,1)}), bf16[8,2,128,512]{3,2,1,0:T(8,128)(2,1)}, u32[]{:S(2)}, u32[]{:S(2)}) async-start(bf16[8,2,128,512]{3,2,1,0:T(8,128)(2,1)} %pack.2), calls=%async_computation | async-start | bytes 4194304 | tf_op jit(solution)/shard_map/all_to_all | solution.py:321
  42.7 47.1 %collective-permute-start.10 = (bf16[4,2,128,512]{3,2,1,0:T(8,128)(2,1)}, bf16[4,2,128,512]{3,2,1,0:T(8,128)(2,1)}, u32[]{:S(2)}, u32[]{:S(2)}) collective-permute-start(bf16[4,2,128,512]{3,2,1,0:T(8,128)(2,1)} %get-tuple-element.294), channel_id=1, source_target_pairs={{0,2},{2,4},{4,6},{1,3},{3,5},{5,7},{8,10},{10,12},{12,14},{9,11},... | collective-permute-start | bytes 3145736 | tf_op jit(solution)/shard_map/ppermute | solution.py:336
  47.2 42.7 %collective-permute-start.11 = (bf16[4,2,128,512]{3,2,1,0:T(8,128)(2,1)}, bf16[4,2,128,512]{3,2,1,0:T(8,128)(2,1)}, u32[]{:S(2)}, u32[]{:S(2)}) collective-permute-start(bf16[4,2,128,512]{3,2,1,0:T(8,128)(2,1)} %get-tuple-element.293), channel_id=1, source_target_pairs={{2,0},{4,2},{6,4},{3,1},{5,3},{7,5},{10,8},{12,10},{14,12},{11,9},... | collective-permute-start | bytes 3145736 | tf_op jit(solution)/shard_map/ppermute | solution.py:337
  68.5 139.9 %collective-permute-start.15 = (bf16[4,2,128,512]{3,2,1,0:T(8,128)(2,1)}, bf16[4,2,128,512]{3,2,1,0:T(8,128)(2,1)}, u32[]{:S(2)}, u32[]{:S(2)}) collective-permute-start(bf16[4,2,128,512]{3,2,1,0:T(8,128)(2,1)} %get-tuple-element.292), channel_id=1, source_target_pairs={{0,2},{2,4},{4,6},{1,3},{3,5},{5,7},{8,10},{10,12},{12,14},{9,11},... | collective-permute-start | bytes 3145736 | tf_op jit(solution)/shard_map/ppermute | solution.py:336
  73.0 135.4 %collective-permute-start.16 = (bf16[4,2,128,512]{3,2,1,0:T(8,128)(2,1)}, bf16[4,2,128,512]{3,2,1,0:T(8,128)(2,1)}, u32[]{:S(2)}, u32[]{:S(2)}) collective-permute-start(bf16[4,2,128,512]{3,2,1,0:T(8,128)(2,1)} %get-tuple-element.291), channel_id=1, source_target_pairs={{2,0},{4,2},{6,4},{3,1},{5,3},{7,5},{10,8},{12,10},{14,12},{11,9},... | collective-permute-start | bytes 3145736 | tf_op jit(solution)/shard_map/ppermute | solution.py:337
  78.4 1.5 collective-permute-start.2
  85.9 1.5 collective-permute-start.2
  102.7 116.8 %all-to-all-start.2 = ((bf16[8,2,128,512]{3,2,1,0:T(8,128)(2,1)}), bf16[8,2,128,512]{3,2,1,0:T(8,128)(2,1)}, u32[]{:S(2)}, u32[]{:S(2)}) async-start(bf16[8,2,128,512]{3,2,1,0:T(8,128)(2,1)} %get-tuple-element.235), calls=%async_computation.2 | async-start | bytes 4194304 | tf_op jit(solution)/shard_map/all_to_all | solution.py:321
  107.1 17.2 %copy-start.1 = (f32[8,8,128]{2,1,0:T(8,128)S(1)}, f32[8,8,128]{2,1,0:T(8,128)}, u32[]{:S(2)}) copy-start(f32[8,8,128]{2,1,0:T(8,128)} %get-tuple-element.238) | copy-start | bytes 98308
  112.1 1.5 collective-permute-start.7
  120.4 1.5 collective-permute-start.7
  124.3 79.0 %collective-permute-start.12 = (f32[8,8,128]{2,1,0:T(8,128)S(1)}, f32[8,8,128]{2,1,0:T(8,128)S(1)}, u32[]{:S(2)}, u32[]{:S(2)}) collective-permute-start(f32[8,8,128]{2,1,0:T(8,128)S(1)} %copy-done.1), channel_id=1, source_target_pairs={{0,2},{2,0},{4,6},{6,4},{1,3},{3,1},{5,7},{7,5},{8,10},{10,8},{12,... | collective-permute-start | bytes 98312 | tf_op jit(solution)/shard_map/ppermute | solution.py:392
  200.9 4.8 %collective-permute-start.13 = (f32[8,8,128]{2,1,0:T(8,128)S(1)}, f32[8,8,128]{2,1,0:T(8,128)S(1)}, u32[]{:S(2)}, u32[]{:S(2)}) collective-permute-start(f32[8,8,128]{2,1,0:T(8,128)S(1)} %copy-done.1), channel_id=1, source_target_pairs={{0,4},{2,6},{4,0},{6,2},{1,5},{3,7},{5,1},{7,3},{8,12},{10,14},{12... | collective-permute-start | bytes 98312 | tf_op jit(solution)/shard_map/ppermute | solution.py:392
  202.0 5.7 %collective-permute-start.14 = (f32[8,8,128]{2,1,0:T(8,128)S(1)}, f32[8,8,128]{2,1,0:T(8,128)S(1)}, u32[]{:S(2)}, u32[]{:S(2)}) collective-permute-start(f32[8,8,128]{2,1,0:T(8,128)S(1)} %copy-done.1), channel_id=1, source_target_pairs={{0,6},{2,4},{4,2},{6,0},{1,7},{3,5},{5,3},{7,1},{8,14},{10,12},{12... | collective-permute-start | bytes 98312 | tf_op jit(solution)/shard_map/ppermute | solution.py:392
  219.5 29.6 %all-to-all-start.3 = ((bf16[8,2,128,512]{3,2,1,0:T(8,128)(2,1)}), bf16[8,2,128,512]{3,2,1,0:T(8,128)(2,1)S(1)}, u32[]{:S(2)}, u32[]{:S(2)}) async-start(bf16[8,2,128,512]{3,2,1,0:T(8,128)(2,1)} %key_pass.1), calls=%async_computation.3 | async-start | bytes 4194304 | tf_op jit(solution)/shard_map/all_to_all | solution.py:321
  249.2 1.3 copy-start

commit v2 on v1

--- a/solution.py
+++ b/solution.py
@@ -17,6 +17,7 @@
 SCALE = HEAD_DIM ** (-0.5)
 SCALE2 = SCALE * math.log2(math.e)
 OWN = 3
+WIDE = 4
 
 
 def head_of(h):
@@ -31,18 +32,23 @@
     return lax.dot_general(a, b, (((1,), (0,)), ((), ())), preferred_element_type=F32)
 
 
-def pack_kernel(a_ref, b_ref, out_ref, sem):
+def pack_kernel(a_ref, b_ref, out_ref, held, in_sem, out_sem):
     groups, _, _, columns = out_ref.shape
-    copies = [
-        pltpu.make_async_copy(
-            source.at[:, c * columns : (c + 1) * columns], out_ref.at[c, n], sem.at[c, n]
-        )
-        for c in range(groups)
-        for n, source in enumerate((a_ref, b_ref))
-    ]
-    for copy in copies:
+    arrive, leave = [], []
+    for c in range(groups):
+        for n, source in enumerate((a_ref, b_ref)):
+            arrive.append(
+                pltpu.make_async_copy(
+                    source.at[:, c * columns : (c + 1) * columns], held.at[c, n], in_sem.at[c, n]
+                )
+            )
+            leave.append(pltpu.make_async_copy(held.at[c, n], out_ref.at[c, n], out_sem.at[c, n]))
+    for copy in arrive:
         copy.start()
-    for copy in copies:
+    for first, second in zip(arrive, leave):
+        first.wait()
+        second.start()
+    for copy in leave:
         copy.wait()
 
 
@@ -63,13 +69,18 @@
 
 def pack(a, b, groups):
     rows, columns = a.shape
+    shape = (groups, 2, rows, columns // groups)
     anywhere = pl.BlockSpec(memory_space=pl.ANY)
     return pl.pallas_call(
         pack_kernel,
-        out_shape=jax.ShapeDtypeStruct((groups, 2, rows, columns // groups), a.dtype),
+        out_shape=jax.ShapeDtypeStruct(shape, a.dtype),
         in_specs=[anywhere] * 2,
-        out_specs=pl.BlockSpec(memory_space=pltpu.VMEM),
-        scratch_shapes=[pltpu.SemaphoreType.DMA((groups, 2))],
+        out_specs=anywhere,
+        scratch_shapes=[
+            pltpu.VMEM(shape, a.dtype),
+            pltpu.SemaphoreType.DMA((groups, 2)),
+            pltpu.SemaphoreType.DMA((groups, 2)),
+        ],
         name="pack",
     )(a, b)
 
@@ -84,6 +95,7 @@
         in_specs=[pl.BlockSpec(memory_space=pltpu.VMEM)],
         out_specs=(anywhere, anywhere),
         scratch_shapes=[pltpu.SemaphoreType.DMA((groups, 2))],
+        compiler_params=pltpu.CompilerParams(vmem_limit_bytes=5 * rows * groups * columns),
         name="unpack",
     )(pair)
 
@@ -98,13 +110,28 @@
     for copy in copies:
         copy.start()
 
+    ahead, rest = extra
+    early = ahead.shape[0]
+
     def move(slot):
-        return pltpu.make_async_copy(extra.at[slot], pool.at[start + slot], extra_sem.at[slot])
-
-    lax.fori_loop(0, count, lambda slot, _: (move(slot).start(), 0)[1], 0)
+        return pltpu.make_async_copy(rest.at[slot - early], pool.at[start + slot], extra_sem.at[slot])
+
+    def move_ahead():
+        return pltpu.make_async_copy(ahead, pool.at[pl.ds(start, early)], extra_sem.at[0])
+
+    @pl.when(count > 0)
+    def _():
+        move_ahead().start()
+
+    lax.fori_loop(early, count, lambda slot, _: (move(slot).start(), 0)[1], 0)
     for copy in copies:
         copy.wait()
-    lax.fori_loop(0, count, lambda slot, _: (move(slot).wait(), 0)[1], 0)
+
+    @pl.when(count > 0)
+    def _():
+        move_ahead().wait()
+
+    lax.fori_loop(early, count, lambda slot, _: (move(slot).wait(), 0)[1], 0)
 
 
 def by_width(cross, width, body):
@@ -125,10 +152,10 @@
 
 
 def query_kernel(
-    width, heads, slot_ref, valid_ref, cross_ref, count_ref, qg_ref, kv_local, below, above, extra,
+    width, heads, slot_ref, valid_ref, cross_ref, count_ref, qg_ref, kv_local, below, above, ahead, rest,
     out_ref, stat_ref, pool, sem, extra_sem,
 ):
-    fill_pool(count_ref[0], (kv_local, below, above), pool, extra, sem, extra_sem)
+    fill_pool(count_ref[0], (kv_local, below, above), pool, (ahead, rest), sem, extra_sem)
     lane = lax.broadcasted_iota(jnp.int32, (BLOCK, BLOCK), 1)
 
     def block(i, _):
@@ -176,9 +203,9 @@
 
 def key_kernel(
     width, heads, slot_ref, valid_ref, place_ref, cross_ref, count_ref, kv_ref, stat_ref, qg_local,
-    below, above, extra, out_ref, pool, sem, extra_sem,
+    below, above, ahead, rest, out_ref, pool, sem, extra_sem,
 ):
-    fill_pool(count_ref[0], (qg_local, below, above), pool, extra, sem, extra_sem)
+    fill_pool(count_ref[0], (qg_local, below, above), pool, (ahead, rest), sem, extra_sem)
 
     def block(j, _):
         def body(count):
@@ -228,8 +255,8 @@
 def tables(block_mask, spans, span_len, steps, groups):
     z = lax.axis_index("z")
     local = spans * SUB
-    most = (spans * (spans - 1) + len(groups)) // 2
-    capacity = 2 * most
+    most = (spans * (spans - 1) + (WIDE - 1) * len(groups)) // WIDE
+    capacity = WIDE * most
     iota = functools.partial(lax.broadcasted_iota, jnp.int32)
     as_int = lambda flags: flags.astype(jnp.int32)
     cube = block_mask.reshape(spans, span_len, spans, span_len)
@@ -245,13 +272,18 @@
     group = jnp.where(hop > 0, base_of(hop, top) + low, -1)
     per_place = group.reshape(spans, steps, SUB, spans)
     numbers = iota((len(groups), spans, steps, SUB, spans), 0)
-    rounds = (jnp.max(jnp.sum(as_int(per_place[None] == numbers), axis=(1, 3, 4)), axis=1) + 1) // 2
+    messages = jnp.max(jnp.sum(as_int(per_place[None] == numbers), axis=(1, 3, 4)), axis=1)
+    rounds = (messages + WIDE - 1) // WIDE
     number = iota((len(groups), len(groups)), 0)
     ends = jnp.sum(jnp.where(number <= iota(number.shape, 1), rounds[:, None], 0), axis=0)
     starts = ends - rounds
     total = jnp.sum(rounds)
     at = iota((most, len(groups)), 0)
     plan = jnp.minimum(jnp.sum(as_int(at >= ends[None]), axis=1), len(groups) - 1)
+    left = jnp.sum(
+        jnp.where(plan[:, None] == iota(at.shape, 1), messages[None] - WIDE * (at - starts[None]), 0), axis=1
+    )
+    plan = 2 * plan + as_int(left <= WIDE // 2)
     key = jnp.where(
         mine < other,
         (mine * span_len + spot) * spans + other,
@@ -272,10 +304,11 @@
     first = jnp.sum(
         jnp.where(flat[:, None] == iota((local * spans, len(groups)), 1), starts[None], 0), axis=1
     )
-    extra_slot = 2 * first + rank
+    extra_slot = WIDE * first + rank
     hits = crossing[:, None] & (extra_slot[:, None] == iota((local * spans, capacity), 1))
-    send_block = jnp.sum(as_int(hits) * block_l.reshape(-1)[:, None], axis=0).reshape(most, 2)
-    plan = (plan * local + send_block[:, 0]) * local + send_block[:, 1]
+    send_block = jnp.sum(as_int(hits) * block_l.reshape(-1)[:, None], axis=0).reshape(most, WIDE)
+    for n in range(WIDE):
+        plan = plan * local + send_block[:, n]
     cross_slot = jnp.where(
         group_l >= 0,
         local + 2 * spans + extra_slot.reshape(local, spans),
@@ -340,29 +373,51 @@
     kv_below, kv_above = neighbours(kv)
     qg_below, qg_above = neighbours(qg)
 
+    def take(code):
+        picks = []
+        for _ in range(WIDE):
+            picks.insert(0, code % local)
+            code = code // local
+        return code, picks
+
+    def swap(pair, *picks, group, size):
+        sent = jnp.concatenate([lax.dynamic_slice_in_dim(pair, n, 1, 0) for n in picks[:size]])
+        got = lax.ppermute(sent, "z", group)
+        return jnp.concatenate([got] * (WIDE // size))
+
+    swaps = [
+        lambda pair, *picks, g=g, n=n: swap(pair, *picks, group=g, size=n)
+        for g in groups
+        for n in (WIDE, WIDE // 2)
+    ]
+    blank = functools.partial(
+        pl.pallas_call,
+        lambda out_ref: None,
+        out_specs=pl.BlockSpec(memory_space=pl.ANY),
+        compiler_params=pltpu.CompilerParams(vmem_limit_bytes=1 << 20),
+        name="extra_blocks",
+    )
+
     def crossing(pair):
-        buffer = pl.pallas_call(
-            lambda out_ref: None,
-            out_shape=jax.ShapeDtypeStruct((capacity, 2, BLOCK, columns), BF16),
-            out_specs=pl.BlockSpec(memory_space=pl.ANY),
-            name="extra_blocks",
-        )()
-        swaps = [functools.partial(lax.ppermute, axis_name="z", perm=g) for g in groups]
+        size = (WIDE, 2, BLOCK, columns)
+        unused = blank(out_shape=jax.ShapeDtypeStruct(size, BF16))()
+        buffer = blank(out_shape=jax.ShapeDtypeStruct((capacity - WIDE,) + size[1:], BF16))()
 
         def one_round(r, held):
-            code = plan[r]
-            first, second = code // local % local, code % local
-            sent = jnp.concatenate(
-                [lax.dynamic_slice_in_dim(pair, n, 1, 0) for n in (first, second)]
-            )
-            got = lax.switch(code // (local * local), swaps, sent)
-            return lax.dynamic_update_slice_in_dim(held, got, 2 * r, 0)
-
-        return lax.fori_loop(0, total, one_round, buffer)
+            code, picks = take(plan[r])
+            got = lax.switch(code // 2, swaps[::2], pair, *picks)
+            return lax.dynamic_update_slice_in_dim(held, got, WIDE * (r - 1), 0)
+
+        code, picks = take(plan[0])
+        skip = [lambda held, pair, *picks: held]
+        some = [lambda held, pair, *picks, f=f: f(pair, *picks) for f in swaps]
+        ahead = lax.switch(
+            jnp.where(total > 0, code + 1, 0), skip + some, unused, pair, *picks
+        )
+        return ahead, lax.fori_loop(1, total, one_round, buffer)
 
     kv_extra = crossing(kv)
-    qg_extra = crossing(qg)
-    count = 2 * total.reshape(1)
+    count = WIDE * total.reshape(1)
 
     smem = pl.BlockSpec(memory_space=pltpu.SMEM)
     vmem = pl.BlockSpec(memory_space=pltpu.VMEM)
@@ -372,6 +427,8 @@
         pltpu.SemaphoreType.DMA((3,)),
         pltpu.SemaphoreType.DMA((capacity,)),
     ]
+    block_bytes = 2 * 2 * BLOCK * columns
+    grant = block_bytes * (capacity + 2 * spans + 6 * local) + (10 << 20)
     cost = pl.CostEstimate(
         flops=2 * 4 * local * heads * width * BLOCK * BLOCK * HEAD_DIM,
         bytes_accessed=16 * local * BLOCK * columns,
@@ -383,23 +440,27 @@
             jax.ShapeDtypeStruct(qg.shape, BF16),
             jax.ShapeDtypeStruct((local, 2 * heads, BLOCK), F32),
         ),
-        in_specs=[smem] * 4 + [vmem] + [anywhere] * 4,
+        in_specs=[smem] * 4 + [vmem] + [anywhere] * 5,
         out_specs=(vmem, vmem),
         scratch_shapes=scratch,
         cost_estimate=cost,
+        compiler_params=pltpu.CompilerParams(vmem_limit_bytes=grant),
         name="query_pass",
-    )(slot, ok, cross, count, qg, kv, kv_below, kv_above, kv_extra)
+    )(slot, ok, cross, count, qg, kv, kv_below, kv_above, *kv_extra)
     far = [lax.ppermute(stats, "z", [(n, n ^ d) for n in range(steps)]) for d in range(1, steps)]
     all_stats = jnp.concatenate([stats] + far)
+    qg_late, all_stats = lax.optimization_barrier((qg, all_stats))
+    qg_extra = crossing(qg_late)
     grad_pair = pl.pallas_call(
         functools.partial(key_kernel, width, heads),
         out_shape=jax.ShapeDtypeStruct(kv.shape, BF16),
-        in_specs=[smem] * 5 + [vmem, vmem] + [anywhere] * 4,
+        in_specs=[smem] * 5 + [vmem, vmem] + [anywhere] * 5,
         out_specs=vmem,
         scratch_shapes=scratch,
         cost_estimate=cost,
+        compiler_params=pltpu.CompilerParams(vmem_limit_bytes=grant),
         name="key_pass",
-    )(slot, ok, place, cross, count, kv, all_stats, qg, qg_below, qg_above, qg_extra)
+    )(slot, ok, place, cross, count, kv, all_stats, qg, qg_below, qg_above, *qg_extra)
     out_back = exchange(out_pair)
     grad_back = exchange(grad_pair)
     attended, grad_query = unpack(out_back)

time: 255 us -> 221 us (0.87)
  the two profiles are of different devices: /device:TPU:0 before, /device:TPU:8 now
where the time goes in v2:
time: 221 us; the launch traced here: 220 us
  waiting for transfers between devices  132 us (60%)
  starting transfers between devices  38 us (17%)
  Pallas kernels  30.9 us (14%)
  local copies, waits for them, and re-layouts  11.2 us (5%)
  other arithmetic  3.51 us (2%)
  between operations  2.79 us (1%)
    ppermute x2, waiting for transfers between devices, swap(): got = lax.ppermute(sent, 'z', group)  65.4 us
    all_to_all x4, waiting for transfers between devices, exchange(): lax.all_to_all(pair, ('blk', 'x'), split_axis=0, concat_axis=0, tiled=True)  43.9 us
    ppermute x3, waiting for transfers between devices, shards(): lax.ppermute(stats, 'z', [(n, n ^ d) for n in range(steps)])  22.9 us
    all_to_all x4, starting transfers between devices, exchange(): lax.all_to_all(pair, ('blk', 'x'), split_axis=0, concat_axis=0, tiled=True)  16.3 us
    pallas_call x1, Pallas kernels, shards(): pl.pallas_call(functools.partial(query_kernel, width, heads), out_shape=(...  11.2 us
    pallas_call x1, Pallas kernels, shards(): pl.pallas_call(functools.partial(key_kernel, width, heads), out_shape=jax...  10 us
    ppermute x2, starting transfers between devices, swap(): got = lax.ppermute(sent, 'z', group)  6.42 us
    ppermute x2, starting transfers between devices, neighbours(): above = lax.ppermute(edges[:, 0], 'z', downward)  6.41 us
  transfers between devices with their start and end apart: 13, of which 7 were waited for; matrix products, arithmetic and copies ran while one was open for 5% of the time, Pallas kernels for 6%

profile of v2, /device:TPU:8, one launch (start us, length us, event | category | flops | bytes accessed | tf_op | source)
XLA Modules:
  0.0 220.1 jit_solution(5287897092390061309)
XLA Ops:
  0.6 2.6 %pack.3 = bf16[8,2,128,512]{3,2,1,0:T(8,128)(2,1)} custom-call(bf16[128,4096]{1,0:T(8,128)(2,1)} %a_ref.3, bf16[128,4096]{1,0:T(8,128)(2,1)} %b_ref.3), custom_call_target="tpu_custom_call" | custom-call | tf_op jit(solution)/shard_map/pack/pallas_call | solution.py:74
  3.2 3.7 %all-to-all-start.1 = ((bf16[8,2,128,512]{3,2,1,0:T(8,128)(2,1)}), bf16[8,2,128,512]{3,2,1,0:T(8,128)(2,1)S(1)}, u32[]{:S(2)}, u32[]{:S(2)}) async-start(bf16[8,2,128,512]{3,2,1,0:T(8,128)(2,1)} %pack.3), calls=%async_computation.1 | async-start | bytes 4194304 | tf_op jit(solution)/shard_map/all_to_all | solution.py:354
  7.2 0.6 multiply_reduce_fusion
  7.8 0.1 fusion.35
  8.1 0.1 fusion.19
  8.3 0.2 compare_select_fusion
  8.7 0.6 fusion.36
  9.6 0.2 convert_reduce_fusion.1
  10.2 0.1 copy.74
  10.5 2.6 %pack.2 = bf16[8,2,128,512]{3,2,1,0:T(8,128)(2,1)} custom-call(bf16[128,4096]{1,0:T(8,128)(2,1)} %a_ref.2, bf16[128,4096]{1,0:T(8,128)(2,1)} %b_ref.2), custom_call_target="tpu_custom_call" | custom-call | tf_op jit(solution)/shard_map/pack/pallas_call | solution.py:74
  13.1 0.1 convert_reduce_fusion.3
  13.2 0.2 slice_reduce_fusion.3
  13.4 0.2 select_reduce_fusion.4
  13.7 19.3 %all-to-all-done.1.kv_local.kv_ref = bf16[8,2,128,512]{3,2,1,0:T(8,128)(2,1)S(1)} async-done(((bf16[8,2,128,512]{3,2,1,0:T(8,128)(2,1)}), bf16[8,2,128,512]{3,2,1,0:T(8,128)(2,1)S(1)}, u32[]{:S(2)}, u32[]{:S(2)}) %all-to-all-start.1) | async-done | bytes 2097184 | tf_op jit(solution)/shard_map/all_to_all | solution.py:354
  33.0 4.3 %all-to-all-start = ((bf16[8,2,128,512]{3,2,1,0:T(8,128)(2,1)}), bf16[8,2,128,512]{3,2,1,0:T(8,128)(2,1)}, u32[]{:S(2)}, u32[]{:S(2)}) async-start(bf16[8,2,128,512]{3,2,1,0:T(8,128)(2,1)} %pack.2), calls=%async_computation | async-start | bytes 4194304 | tf_op jit(solution)/shard_map/all_to_all | solution.py:354
  37.4 0.1 copy.72
  37.7 1.2 slice_bitcast_fusion.2
  38.9 3.5 %collective-permute-start.30 = (bf16[4,2,128,512]{3,2,1,0:T(8,128)(2,1)}, bf16[4,2,128,512]{3,2,1,0:T(8,128)(2,1)S(1)}, u32[]{:S(2)}, u32[]{:S(2)}) collective-permute-start(bf16[4,2,128,512]{3,2,1,0:T(8,128)(2,1)} %get-tuple-element.810), channel_id=1, source_target_pairs={{0,2},{2,4},{4,6},{1,3},{3,5},{5,7},{8,10},{10,12},{12,14},{9,11},... | collective-permute-start | bytes 3145736 | tf_op jit(solution)/shard_map/ppermute | solution.py:369
  42.4 2.4 %collective-permute-start.31 = (bf16[4,2,128,512]{3,2,1,0:T(8,128)(2,1)S(1)}, bf16[4,2,128,512]{3,2,1,0:T(8,128)(2,1)S(1)}, u32[]{:S(2)}, u32[]{:S(2)}) collective-permute-start(bf16[4,2,128,512]{3,2,1,0:T(8,128)(2,1)S(1)} %get-tuple-element.809), channel_id=1, source_target_pairs={{2,0},{4,2},{6,4},{3,1},{5,3},{7,5},{10,8},{12,10},{14,12},{11,9},... | collective-permute-start | bytes 3145736 | tf_op jit(solution)/shard_map/ppermute | solution.py:370
  47.1 46.0 %conditional.4 = (bf16[4,2,128,512]{3,2,1,0:T(8,128)(2,1)}) conditional(s32[]{:T(128)} %clamp.18, bf16[4,2,128,512]{3,2,1,0:T(8,128)(2,1)} %extra_blocks.4, (s32[]{:T(128)}, bf16[8,2,128,512]{3,2,1,0:T(8,128)(2,1)}, s32[]{:T(128)}, s32[]{:T(128)}, s32[]{:T(128)}) %tuple.300, (s32[]{:T(128)}, ...), branch_computations={%region_14.15_spmd, %region_15.16_spmd, %region_16.17_spmd, %regio... | conditional | flops 1572876 | bytes 8388808 | solution.py:414
  47.1 1.3 constant_dynamic-slice_fusion.15
  48.4 0.1 pad_maximum_fusion.6
  48.5 4.5 %collective-permute-start.4 = (bf16[4,2,128,512]{3,2,1,0:T(8,128)(2,1)S(1)}, bf16[4,2,128,512]{3,2,1,0:T(8,128)(2,1)}, u32[]{:S(2)}, u32[]{:S(2)}) collective-permute-start(bf16[4,2,128,512]{3,2,1,0:T(8,128)(2,1)S(1)} %pad_maximum_fusion.6), channel_id=1, source_target_pairs={{2,6},{6,2},{3,7},{7,3},{10,14},{14,10},{11,15},{15,11},{18,22},{2... | collective-permute-start | bytes 3145736 | tf_op jit(solution)/shard_map/cond/branch_5_fun/ppermute | solution.py:385
  53.0 40.0 %collective-permute-done.4 = bf16[4,2,128,512]{3,2,1,0:T(8,128)(2,1)} collective-permute-done((bf16[4,2,128,512]{3,2,1,0:T(8,128)(2,1)S(1)}, bf16[4,2,128,512]{3,2,1,0:T(8,128)(2,1)}, u32[]{:S(2)}, u32[]{:S(2)}) %collective-permute-start.4) | collective-permute-done | bytes 1048608 | tf_op jit(solution)/shard_map/cond/branch_5_fun/ppermute | solution.py:385
  93.0 0.7 while.26
  93.7 11.2 %query_pass.1 = (bf16[8,2,128,512]{3,2,1,0:T(8,128)(2,1)S(1)}, f32[8,8,128]{2,1,0:T(8,128)S(1)}) custom-call(s32[8,6]{1,0:T(8,128)S(1)} %add_select_fusion.5.slot_ref, s32[8,6]{1,0:T(8,128)S(1)} %get-tuple-element.689.valid_ref, s32[8]{0:T(128)S(1)} %reduce_sum.137.cross_ref, s32[1]{0:T(128)} %bitcast.4.count_ref, ...), custom_call_target="tpu_custom_call" | custom-call | flops 3221225472 | bytes 8388608 | tf_op jit(solution)/shard_map/query_pass/pallas_call | solution.py:437
  105.0 1.3 copy-done.1
  106.2 3.8 %all-to-all-start.2 = ((bf16[8,2,128,512]{3,2,1,0:T(8,128)(2,1)}), bf16[8,2,128,512]{3,2,1,0:T(8,128)(2,1)S(1)}, u32[]{:S(2)}, u32[]{:S(2)}) async-start(bf16[8,2,128,512]{3,2,1,0:T(8,128)(2,1)} %copy-done.1), calls=%async_computation.2 | async-start | bytes 4194304 | tf_op jit(solution)/shard_map/all_to_all | solution.py:354
  110.1 3.0 %slice_bitcast_fusion = (bf16[4,2,128,512]{3,2,1,0:T(8,128)(2,1)}, bf16[4,2,128,512]{3,2,1,0:T(8,128)(2,1)}) fusion(bf16[4,2,2,128,512]{4,3,2,1,0:T(8,128)(2,1)} %bitcast.9), kind=kLoop, calls=%fused_computation.142 | loop fusion | bytes 4194304 | tf_op jit(solution)/shard_map/squeeze | solution.py:370
  113.1 1.9 collective-permute-start.35
  115.0 4.0 %collective-permute-start.36 = (bf16[4,2,128,512]{3,2,1,0:T(8,128)(2,1)}, bf16[4,2,128,512]{3,2,1,0:T(8,128)(2,1)}, u32[]{:S(2)}, u32[]{:S(2)}) collective-permute-start(bf16[4,2,128,512]{3,2,1,0:T(8,128)(2,1)} %get-tuple-element.807), channel_id=1, source_target_pairs={{2,0},{4,2},{6,4},{3,1},{5,3},{7,5},{10,8},{12,10},{14,12},{11,9},... | collective-permute-start | bytes 3145736 | tf_op jit(solution)/shard_map/ppermute | solution.py:370
  119.1 1.4 collective-permute-start.33
  120.5 2.1 collective-permute-start.34
  122.6 21.0 %collective-permute-done.32 = f32[8,8,128]{2,1,0:T(8,128)S(1)} collective-permute-done((f32[8,8,128]{2,1,0:T(8,128)S(1)}, f32[8,8,128]{2,1,0:T(8,128)S(1)}, u32[]{:S(2)}, u32[]{:S(2)}) %collective-permute-start.32) | collective-permute-done | bytes 32800 | tf_op jit(solution)/shard_map/ppermute | solution.py:450
  143.6 0.9 collective-permute-done.33
  144.5 1.1 collective-permute-done.34
  145.5 28.8 %conditional.5 = (bf16[4,2,128,512]{3,2,1,0:T(8,128)(2,1)}) conditional(s32[]{:T(128)} %clamp.18, bf16[4,2,128,512]{3,2,1,0:T(8,128)(2,1)} %extra_blocks.6, (s32[]{:T(128)}, bf16[8,2,128,512]{3,2,1,0:T(8,128)(2,1)}, s32[]{:T(128)}, s32[]{:T(128)}, s32[]{:T(128)}) %tuple.139, (s32[]{:T(128)}, ...), branch_computations={%region_33.34_spmd, %region_34.35_spmd, %region_35.36_spmd, %regio... | conditional | flops 1572876 | bytes 8388808 | solution.py:414
  145.6 1.3 constant_dynamic-slice_fusion.65
  146.9 0.1 pad_maximum_fusion.26
  147.1 1.9 collective-permute-start.19
  149.0 25.4 %collective-permute-done.19 = bf16[4,2,128,512]{3,2,1,0:T(8,128)(2,1)} collective-permute-done((bf16[4,2,128,512]{3,2,1,0:T(8,128)(2,1)S(1)}, bf16[4,2,128,512]{3,2,1,0:T(8,128)(2,1)}, u32[]{:S(2)}, u32[]{:S(2)}) %collective-permute-start.19) | collective-permute-done | bytes 1048608 | tf_op jit(solution)/shard_map/cond/branch_5_fun/ppermute | solution.py:385
  174.4 0.7 while.27
  175.1 10.0 %key_pass.1 = bf16[8,2,128,512]{3,2,1,0:T(8,128)(2,1)S(1)} custom-call(s32[8,6]{1,0:T(8,128)S(1)} %add_select_fusion.5.slot_ref, s32[8,6]{1,0:T(8,128)S(1)} %get-tuple-element.689.valid_ref, s32[8,6]{1,0:T(8,128)S(1)} %get-tuple-element.687.place_ref, s32[8]{0:T(128)S(1)} %reduce_sum.137.cross_ref, s32[1]{0:T(128)} %bitcast.4.count_ref, ...), custom_call_target="tpu_custom_call" | custom-call | flops 3221225472 | bytes 8388608 | tf_op jit(solution)/shard_map/key_pass/pallas_call | solution.py:454
  185.1 1.3 copy-done
  186.4 4.4 %all-to-all-start.3 = ((bf16[8,2,128,512]{3,2,1,0:T(8,128)(2,1)}), bf16[8,2,128,512]{3,2,1,0:T(8,128)(2,1)}, u32[]{:S(2)}, u32[]{:S(2)}) async-start(bf16[8,2,128,512]{3,2,1,0:T(8,128)(2,1)} %copy-done), calls=%async_computation.3 | async-start | bytes 4194304 | tf_op jit(solution)/shard_map/all_to_all | solution.py:354
  190.8 1.4 unpack.2
  192.2 24.6 %all-to-all-done.3.in_ref = bf16[8,2,128,512]{3,2,1,0:T(8,128)(2,1)} async-done(((bf16[8,2,128,512]{3,2,1,0:T(8,128)(2,1)}), bf16[8,2,128,512]{3,2,1,0:T(8,128)(2,1)}, u32[]{:S(2)}, u32[]{:S(2)}) %all-to-all-start.3) | async-done | bytes 2097184 | tf_op jit(solution)/shard_map/all_to_all | solution.py:354
  216.8 3.0 %unpack.3 = (bf16[128,4096]{1,0:T(8,128)(2,1)}, bf16[128,4096]{1,0:T(8,128)(2,1)}) custom-call(bf16[8,2,128,512]{3,2,1,0:T(8,128)(2,1)} %all-to-all-done.3.in_ref), custom_call_target="tpu_custom_call" | custom-call | tf_op jit(solution)/shard_map/unpack/pallas_call | solution.py:92
  (71 shorter events, 2.4 us)
Async XLA Ops:
  3.2 3.8 %copy-start.3 = (s32[32,32]{1,0:T(8,128)S(1)}, s32[32,32]{1,0:T(8,128)}, u32[]{:S(2)}) copy-start(s32[32,32]{1,0:T(8,128)} %param.45) | copy-start | bytes 12292
  3.2 29.8 %all-to-all-start.1 = ((bf16[8,2,128,512]{3,2,1,0:T(8,128)(2,1)}), bf16[8,2,128,512]{3,2,1,0:T(8,128)(2,1)S(1)}, u32[]{:S(2)}, u32[]{:S(2)}) async-start(bf16[8,2,128,512]{3,2,1,0:T(8,128)(2,1)} %pack.3), calls=%async_computation.1 | async-start | bytes 4194304 | tf_op jit(solution)/shard_map/all_to_all | solution.py:354
  33.0 4.7 %copy-start.2 = (bf16[8,2,128,512]{3,2,1,0:T(8,128)(2,1)}, bf16[8,2,128,512]{3,2,1,0:T(8,128)(2,1)S(1)}, u32[]{:S(2)}) copy-start(bf16[8,2,128,512]{3,2,1,0:T(8,128)(2,1)S(1)} %all-to-all-done.1.kv_local.kv_ref) | copy-start | bytes 6291460
  33.0 60.7 %all-to-all-start = ((bf16[8,2,128,512]{3,2,1,0:T(8,128)(2,1)}), bf16[8,2,128,512]{3,2,1,0:T(8,128)(2,1)}, u32[]{:S(2)}, u32[]{:S(2)}) async-start(bf16[8,2,128,512]{3,2,1,0:T(8,128)(2,1)} %pack.2), calls=%async_computation | async-start | bytes 4194304 | tf_op jit(solution)/shard_map/all_to_all | solution.py:354
  38.9 54.8 %collective-permute-start.30 = (bf16[4,2,128,512]{3,2,1,0:T(8,128)(2,1)}, bf16[4,2,128,512]{3,2,1,0:T(8,128)(2,1)S(1)}, u32[]{:S(2)}, u32[]{:S(2)}) collective-permute-start(bf16[4,2,128,512]{3,2,1,0:T(8,128)(2,1)} %get-tuple-element.810), channel_id=1, source_target_pairs={{0,2},{2,4},{4,6},{1,3},{3,5},{5,7},{8,10},{10,12},{12,14},{9,11},... | collective-permute-start | bytes 3145736 | tf_op jit(solution)/shard_map/ppermute | solution.py:369
  42.4 51.3 %collective-permute-start.31 = (bf16[4,2,128,512]{3,2,1,0:T(8,128)(2,1)S(1)}, bf16[4,2,128,512]{3,2,1,0:T(8,128)(2,1)S(1)}, u32[]{:S(2)}, u32[]{:S(2)}) collective-permute-start(bf16[4,2,128,512]{3,2,1,0:T(8,128)(2,1)S(1)} %get-tuple-element.809), channel_id=1, source_target_pairs={{2,0},{4,2},{6,4},{3,1},{5,3},{7,5},{10,8},{12,10},{14,12},{11,9},... | collective-permute-start | bytes 3145736 | tf_op jit(solution)/shard_map/ppermute | solution.py:370
  48.5 44.5 %collective-permute-start.4 = (bf16[4,2,128,512]{3,2,1,0:T(8,128)(2,1)S(1)}, bf16[4,2,128,512]{3,2,1,0:T(8,128)(2,1)}, u32[]{:S(2)}, u32[]{:S(2)}) collective-permute-start(bf16[4,2,128,512]{3,2,1,0:T(8,128)(2,1)S(1)} %pad_maximum_fusion.6), channel_id=1, source_target_pairs={{2,6},{6,2},{3,7},{7,3},{10,14},{14,10},{11,15},{15,11},{18,22},{2... | collective-permute-start | bytes 3145736 | tf_op jit(solution)/shard_map/cond/branch_5_fun/ppermute | solution.py:385
  105.0 1.3 copy-start.1
  106.2 80.2 %all-to-all-start.2 = ((bf16[8,2,128,512]{3,2,1,0:T(8,128)(2,1)}), bf16[8,2,128,512]{3,2,1,0:T(8,128)(2,1)S(1)}, u32[]{:S(2)}, u32[]{:S(2)}) async-start(bf16[8,2,128,512]{3,2,1,0:T(8,128)(2,1)} %copy-done.1), calls=%async_computation.2 | async-start | bytes 4194304 | tf_op jit(solution)/shard_map/all_to_all | solution.py:354
  113.1 61.9 %collective-permute-start.35 = (bf16[4,2,128,512]{3,2,1,0:T(8,128)(2,1)}, bf16[4,2,128,512]{3,2,1,0:T(8,128)(2,1)S(1)}, u32[]{:S(2)}, u32[]{:S(2)}) collective-permute-start(bf16[4,2,128,512]{3,2,1,0:T(8,128)(2,1)} %get-tuple-element.808), channel_id=1, source_target_pairs={{0,2},{2,4},{4,6},{1,3},{3,5},{5,7},{8,10},{10,12},{12,14},{9,11},... | collective-permute-start | bytes 3145736 | tf_op jit(solution)/shard_map/ppermute | solution.py:369
  115.0 60.0 %collective-permute-start.36 = (bf16[4,2,128,512]{3,2,1,0:T(8,128)(2,1)}, bf16[4,2,128,512]{3,2,1,0:T(8,128)(2,1)}, u32[]{:S(2)}, u32[]{:S(2)}) collective-permute-start(bf16[4,2,128,512]{3,2,1,0:T(8,128)(2,1)} %get-tuple-element.807), channel_id=1, source_target_pairs={{2,0},{4,2},{6,4},{3,1},{5,3},{7,5},{10,8},{12,10},{14,12},{11,9},... | collective-permute-start | bytes 3145736 | tf_op jit(solution)/shard_map/ppermute | solution.py:370
  119.0 24.6 %collective-permute-start.32 = (f32[8,8,128]{2,1,0:T(8,128)S(1)}, f32[8,8,128]{2,1,0:T(8,128)S(1)}, u32[]{:S(2)}, u32[]{:S(2)}) collective-permute-start(f32[8,8,128]{2,1,0:T(8,128)S(1)} %get-tuple-element.654), channel_id=1, source_target_pairs={{0,2},{2,0},{4,6},{6,4},{1,3},{3,1},{5,7},{7,5},{8,10},{10,8},{12,... | collective-permute-start | bytes 98312 | tf_op jit(solution)/shard_map/ppermute | solution.py:450
  119.1 25.4 %collective-permute-start.33 = (f32[8,8,128]{2,1,0:T(8,128)S(1)}, f32[8,8,128]{2,1,0:T(8,128)S(1)}, u32[]{:S(2)}, u32[]{:S(2)}) collective-permute-start(f32[8,8,128]{2,1,0:T(8,128)S(1)} %get-tuple-element.654), channel_id=1, source_target_pairs={{0,4},{2,6},{4,0},{6,2},{1,5},{3,7},{5,1},{7,3},{8,12},{10,14},{12... | collective-permute-start | bytes 98312 | tf_op jit(solution)/shard_map/ppermute | solution.py:450
  120.5 25.0 %collective-permute-start.34 = (f32[8,8,128]{2,1,0:T(8,128)S(1)}, f32[8,8,128]{2,1,0:T(8,128)S(1)}, u32[]{:S(2)}, u32[]{:S(2)}) collective-permute-start(f32[8,8,128]{2,1,0:T(8,128)S(1)} %get-tuple-element.654), channel_id=1, source_target_pairs={{0,6},{2,4},{4,2},{6,0},{1,7},{3,5},{5,3},{7,1},{8,14},{10,12},{12... | collective-permute-start | bytes 98312 | tf_op jit(solution)/shard_map/ppermute | solution.py:450
  147.1 27.3 %collective-permute-start.19 = (bf16[4,2,128,512]{3,2,1,0:T(8,128)(2,1)S(1)}, bf16[4,2,128,512]{3,2,1,0:T(8,128)(2,1)}, u32[]{:S(2)}, u32[]{:S(2)}) collective-permute-start(bf16[4,2,128,512]{3,2,1,0:T(8,128)(2,1)S(1)} %pad_maximum_fusion.26), channel_id=1, source_target_pairs={{2,6},{6,2},{3,7},{7,3},{10,14},{14,10},{11,15},{15,11},{18,22},{2... | collective-permute-start | bytes 3145736 | tf_op jit(solution)/shard_map/cond/branch_5_fun/ppermute | solution.py:385
  185.1 1.3 copy-start
  186.4 30.4 %all-to-all-start.3 = ((bf16[8,2,128,512]{3,2,1,0:T(8,128)(2,1)}), bf16[8,2,128,512]{3,2,1,0:T(8,128)(2,1)}, u32[]{:S(2)}, u32[]{:S(2)}) async-start(bf16[8,2,128,512]{3,2,1,0:T(8,128)(2,1)} %copy-done), calls=%async_computation.3 | async-start | bytes 4194304 | tf_op jit(solution)/shard_map/all_to_all | solution.py:354

commit v3 on v2

--- a/solution.py
+++ b/solution.py
@@ -405,7 +405,7 @@
 
         def one_round(r, held):
             code, picks = take(plan[r])
-            got = lax.switch(code // 2, swaps[::2], pair, *picks)
+            got = lax.switch(code, swaps, pair, *picks)
             return lax.dynamic_update_slice_in_dim(held, got, WIDE * (r - 1), 0)
 
         code, picks = take(plan[0])
@@ -449,8 +449,7 @@
     )(slot, ok, cross, count, qg, kv, kv_below, kv_above, *kv_extra)
     far = [lax.ppermute(stats, "z", [(n, n ^ d) for n in range(steps)]) for d in range(1, steps)]
     all_stats = jnp.concatenate([stats] + far)
-    qg_late, all_stats = lax.optimization_barrier((qg, all_stats))
-    qg_extra = crossing(qg_late)
+    qg_extra = crossing(qg)
     grad_pair = pl.pallas_call(
         functools.partial(key_kernel, width, heads),
         out_shape=jax.ShapeDtypeStruct(kv.shape, BF16),

time: 221 us -> 221 us (level)
  the two profiles are of different devices: /device:TPU:8 before, /device:TPU:0 now
where the time goes in v3:
time: 221 us; the launch traced here: 220 us
  starting transfers between devices  103 us (47%)
  waiting for transfers between devices  66.6 us (30%)
  Pallas kernels  31.6 us (14%)
  local copies, waits for them, and re-layouts  11.6 us (5%)
  other arithmetic  3.51 us (2%)
  between operations  2.78 us (1%)
    all_to_all x4, waiting for transfers between devices, exchange(): lax.all_to_all(pair, ('blk', 'x'), split_axis=0, concat_axis=0, tiled=True)  57.3 us
    ppermute x3, starting transfers between devices, shards(): lax.ppermute(stats, 'z', [(n, n ^ d) for n in range(steps)])  48 us
    ppermute x2, starting transfers between devices, neighbours(): below = lax.ppermute(edges[:, SUB - 1], 'z', upward)  30.9 us
    all_to_all x4, starting transfers between devices, exchange(): lax.all_to_all(pair, ('blk', 'x'), split_axis=0, concat_axis=0, tiled=True)  17.8 us
    pallas_call x1, Pallas kernels, shards(): pl.pallas_call(functools.partial(query_kernel, width, heads), out_shape=(...  11.6 us
    pallas_call x1, Pallas kernels, shards(): pl.pallas_call(functools.partial(key_kernel, width, heads), out_shape=jax...  10.3 us
    pallas_call x2, Pallas kernels, pack(): pl.pallas_call(pack_kernel, out_shape=jax.ShapeDtypeStruct(shape, a.dtype...  5.22 us
    pallas_call x2, Pallas kernels, unpack(): pl.pallas_call(unpack_kernel, out_shape=(flat, flat), in_specs=[pl.BlockS...  4.47 us
  transfers between devices with their start and end apart: 13, of which 7 were waited for; matrix products, arithmetic and copies ran while one was open for 6% of the time, Pallas kernels for 7%

profile of v3, /device:TPU:0, one launch (start us, length us, event | category | flops | bytes accessed | tf_op | source)
XLA Modules:
  0.0 220.4 jit_solution(10144681283644351576)
XLA Ops:
  0.6 2.6 %pack.3 = bf16[8,2,128,512]{3,2,1,0:T(8,128)(2,1)} custom-call(bf16[128,4096]{1,0:T(8,128)(2,1)} %a_ref.3, bf16[128,4096]{1,0:T(8,128)(2,1)} %b_ref.3), custom_call_target="tpu_custom_call" | custom-call | tf_op jit(solution)/shard_map/pack/pallas_call | solution.py:74
  3.2 5.2 %all-to-all-start.1 = ((bf16[8,2,128,512]{3,2,1,0:T(8,128)(2,1)}), bf16[8,2,128,512]{3,2,1,0:T(8,128)(2,1)S(1)}, u32[]{:S(2)}, u32[]{:S(2)}) async-start(bf16[8,2,128,512]{3,2,1,0:T(8,128)(2,1)} %pack.3), calls=%async_computation.1 | async-start | bytes 4194304 | tf_op jit(solution)/shard_map/all_to_all | solution.py:354
  8.6 0.6 multiply_reduce_fusion
  9.3 0.1 fusion.35
  9.6 0.1 fusion.19
  9.8 0.2 compare_select_fusion
  10.2 0.6 fusion.36
  11.1 0.2 convert_reduce_fusion.1
  11.7 0.1 copy.74
  12.0 2.6 %pack.2 = bf16[8,2,128,512]{3,2,1,0:T(8,128)(2,1)} custom-call(bf16[128,4096]{1,0:T(8,128)(2,1)} %a_ref.2, bf16[128,4096]{1,0:T(8,128)(2,1)} %b_ref.2), custom_call_target="tpu_custom_call" | custom-call | tf_op jit(solution)/shard_map/pack/pallas_call | solution.py:74
  14.6 0.1 convert_reduce_fusion.3
  14.7 0.2 slice_reduce_fusion.3
  14.9 0.2 select_reduce_fusion.4
  15.2 19.2 %all-to-all-done.1.kv_local.kv_ref = bf16[8,2,128,512]{3,2,1,0:T(8,128)(2,1)S(1)} async-done(((bf16[8,2,128,512]{3,2,1,0:T(8,128)(2,1)}), bf16[8,2,128,512]{3,2,1,0:T(8,128)(2,1)S(1)}, u32[]{:S(2)}, u32[]{:S(2)}) %all-to-all-start.1) | async-done | bytes 2097184 | tf_op jit(solution)/shard_map/all_to_all | solution.py:354
  34.5 4.3 %all-to-all-start = ((bf16[8,2,128,512]{3,2,1,0:T(8,128)(2,1)}), bf16[8,2,128,512]{3,2,1,0:T(8,128)(2,1)}, u32[]{:S(2)}, u32[]{:S(2)}) async-start(bf16[8,2,128,512]{3,2,1,0:T(8,128)(2,1)} %pack.2), calls=%async_computation | async-start | bytes 4194304 | tf_op jit(solution)/shard_map/all_to_all | solution.py:354
  38.9 0.1 copy.72
  39.2 1.2 slice_bitcast_fusion.2
  40.4 3.5 %collective-permute-start.40 = (bf16[4,2,128,512]{3,2,1,0:T(8,128)(2,1)}, bf16[4,2,128,512]{3,2,1,0:T(8,128)(2,1)S(1)}, u32[]{:S(2)}, u32[]{:S(2)}) collective-permute-start(bf16[4,2,128,512]{3,2,1,0:T(8,128)(2,1)} %get-tuple-element.1178), channel_id=1, source_target_pairs={{0,2},{2,4},{4,6},{1,3},{3,5},{5,7},{8,10},{10,12},{12,14},{9,11},... | collective-permute-start | bytes 3145736 | tf_op jit(solution)/shard_map/ppermute | solution.py:369
  43.9 1.3 collective-permute-start.41
  47.5 3.3 %conditional.4 = (bf16[4,2,128,512]{3,2,1,0:T(8,128)(2,1)}) conditional(s32[]{:T(128)} %clamp.18, bf16[4,2,128,512]{3,2,1,0:T(8,128)(2,1)} %extra_blocks.4, (s32[]{:T(128)}, bf16[8,2,128,512]{3,2,1,0:T(8,128)(2,1)}, s32[]{:T(128)}, s32[]{:T(128)}, s32[]{:T(128)}) %tuple.368, (s32[]{:T(128)}, ...), branch_computations={%region_14.15_spmd, %region_15.16_spmd, %region_16.17_spmd, %regio... | conditional | flops 1572876 | bytes 8388808 | solution.py:414
  47.5 1.5 constant_dynamic-slice_fusion.15
  49.0 0.1 pad_maximum_fusion.6
  49.1 1.7 collective-permute-start.4
  50.8 0.7 while.26
  51.5 13.4 %all-to-all-done.qg_ref.qg_local = bf16[8,2,128,512]{3,2,1,0:T(8,128)(2,1)} async-done(((bf16[8,2,128,512]{3,2,1,0:T(8,128)(2,1)}), bf16[8,2,128,512]{3,2,1,0:T(8,128)(2,1)}, u32[]{:S(2)}, u32[]{:S(2)}) %all-to-all-start) | async-done | bytes 2097184 | tf_op jit(solution)/shard_map/all_to_all | solution.py:354
  64.9 2.2 %collective-permute-done.40.below = bf16[4,2,128,512]{3,2,1,0:T(8,128)(2,1)S(1)} collective-permute-done((bf16[4,2,128,512]{3,2,1,0:T(8,128)(2,1)}, bf16[4,2,128,512]{3,2,1,0:T(8,128)(2,1)S(1)}, u32[]{:S(2)}, u32[]{:S(2)}) %collective-permute-start.40) | collective-permute-done | bytes 1048608 | tf_op jit(solution)/shard_map/ppermute | solution.py:369
  67.1 3.9 %collective-permute-done.41.above = bf16[4,2,128,512]{3,2,1,0:T(8,128)(2,1)S(1)} collective-permute-done((bf16[4,2,128,512]{3,2,1,0:T(8,128)(2,1)S(1)}, bf16[4,2,128,512]{3,2,1,0:T(8,128)(2,1)S(1)}, u32[]{:S(2)}, u32[]{:S(2)}) %collective-permute-start.41) | collective-permute-done | bytes 1048608 | tf_op jit(solution)/shard_map/ppermute | solution.py:370
  71.0 11.6 %query_pass.1 = (bf16[8,2,128,512]{3,2,1,0:T(8,128)(2,1)S(1)}, f32[8,8,128]{2,1,0:T(8,128)S(1)}) custom-call(s32[8,6]{1,0:T(8,128)S(1)} %add_select_fusion.5.slot_ref, s32[8,6]{1,0:T(8,128)S(1)} %get-tuple-element.1037.valid_ref, s32[8]{0:T(128)S(1)} %reduce_sum.137.cross_ref, s32[1]{0:T(128)} %bitcast.4.count_ref, ...), custom_call_target="tpu_custom_call" | custom-call | flops 3221225472 | bytes 8388608 | tf_op jit(solution)/shard_map/query_pass/pallas_call | solution.py:437
  82.6 1.3 copy-done.1
  83.9 3.8 %all-to-all-start.2 = ((bf16[8,2,128,512]{3,2,1,0:T(8,128)(2,1)}), bf16[8,2,128,512]{3,2,1,0:T(8,128)(2,1)S(1)}, u32[]{:S(2)}, u32[]{:S(2)}) async-start(bf16[8,2,128,512]{3,2,1,0:T(8,128)(2,1)} %copy-done.1), calls=%async_computation.2 | async-start | bytes 4194304 | tf_op jit(solution)/shard_map/all_to_all | solution.py:354
  87.7 3.0 %slice_bitcast_fusion = (bf16[4,2,128,512]{3,2,1,0:T(8,128)(2,1)}, bf16[4,2,128,512]{3,2,1,0:T(8,128)(2,1)}) fusion(bf16[4,2,2,128,512]{4,3,2,1,0:T(8,128)(2,1)} %bitcast.9), kind=kLoop, calls=%fused_computation.182 | loop fusion | bytes 4194304 | tf_op jit(solution)/shard_map/squeeze | solution.py:370
  90.8 27.4 %collective-permute-start.45 = (bf16[4,2,128,512]{3,2,1,0:T(8,128)(2,1)}, bf16[4,2,128,512]{3,2,1,0:T(8,128)(2,1)S(1)}, u32[]{:S(2)}, u32[]{:S(2)}) collective-permute-start(bf16[4,2,128,512]{3,2,1,0:T(8,128)(2,1)} %get-tuple-element.1176), channel_id=1, source_target_pairs={{0,2},{2,4},{4,6},{1,3},{3,5},{5,7},{8,10},{10,12},{12,14},{9,11},... | collective-permute-start | bytes 3145736 | tf_op jit(solution)/shard_map/ppermute | solution.py:369
  118.2 1.3 collective-permute-start.46
  119.5 3.3 %conditional.5 = (bf16[4,2,128,512]{3,2,1,0:T(8,128)(2,1)}) conditional(s32[]{:T(128)} %clamp.18, bf16[4,2,128,512]{3,2,1,0:T(8,128)(2,1)} %extra_blocks.6, (s32[]{:T(128)}, bf16[8,2,128,512]{3,2,1,0:T(8,128)(2,1)}, s32[]{:T(128)}, s32[]{:T(128)}, s32[]{:T(128)}) %tuple.183, (s32[]{:T(128)}, ...), branch_computations={%region_38.39_spmd, %region_39.40_spmd, %region_40.41_spmd, %regio... | conditional | flops 1572876 | bytes 8388808 | solution.py:414
  119.6 1.5 constant_dynamic-slice_fusion.75
  121.1 0.1 pad_maximum_fusion.36
  121.2 1.6 collective-permute-start.24
  122.8 0.9 while.27
  123.7 45.6 %collective-permute-start.42 = (f32[8,8,128]{2,1,0:T(8,128)S(1)}, f32[8,8,128]{2,1,0:T(8,128)S(1)}, u32[]{:S(2)}, u32[]{:S(2)}) collective-permute-start(f32[8,8,128]{2,1,0:T(8,128)S(1)} %get-tuple-element.1004), channel_id=1, source_target_pairs={{0,2},{2,0},{4,6},{6,4},{1,3},{3,1},{5,7},{7,5},{8,10},{10,8},{12,... | collective-permute-start | bytes 98312 | tf_op jit(solution)/shard_map/ppermute | solution.py:450
  169.3 2.4 %collective-permute-start.44 = (f32[8,8,128]{2,1,0:T(8,128)S(1)}, f32[8,8,128]{2,1,0:T(8,128)S(1)}, u32[]{:S(2)}, u32[]{:S(2)}) collective-permute-start(f32[8,8,128]{2,1,0:T(8,128)S(1)} %get-tuple-element.1004), channel_id=1, source_target_pairs={{0,6},{2,4},{4,2},{6,0},{1,7},{3,5},{5,3},{7,1},{8,14},{10,12},{12... | collective-permute-start | bytes 98312 | tf_op jit(solution)/shard_map/ppermute | solution.py:450
  171.8 2.4 %collective-permute-done.43 = f32[8,8,128]{2,1,0:T(8,128)S(1)} collective-permute-done((f32[8,8,128]{2,1,0:T(8,128)S(1)}, f32[8,8,128]{2,1,0:T(8,128)S(1)}, u32[]{:S(2)}, u32[]{:S(2)}) %collective-permute-start.43) | collective-permute-done | bytes 32800 | tf_op jit(solution)/shard_map/ppermute | solution.py:450
  174.1 0.9 collective-permute-done.44
  175.1 10.3 %key_pass.1 = bf16[8,2,128,512]{3,2,1,0:T(8,128)(2,1)S(1)} custom-call(s32[8,6]{1,0:T(8,128)S(1)} %add_select_fusion.5.slot_ref, s32[8,6]{1,0:T(8,128)S(1)} %get-tuple-element.1037.valid_ref, s32[8,6]{1,0:T(8,128)S(1)} %get-tuple-element.1035.place_ref, s32[8]{0:T(128)S(1)} %reduce_sum.137.cross_ref, s32[1]{0:T(128)} %bitcast.4.count_ref, ...), custom_call_target="tpu_custom_call" | custom-call | flops 3221225472 | bytes 8388608 | tf_op jit(solution)/shard_map/key_pass/pallas_call | solution.py:453
  185.4 1.3 copy-done
  186.7 4.4 %all-to-all-start.3 = ((bf16[8,2,128,512]{3,2,1,0:T(8,128)(2,1)}), bf16[8,2,128,512]{3,2,1,0:T(8,128)(2,1)}, u32[]{:S(2)}, u32[]{:S(2)}) async-start(bf16[8,2,128,512]{3,2,1,0:T(8,128)(2,1)} %copy-done), calls=%async_computation.3 | async-start | bytes 4194304 | tf_op jit(solution)/shard_map/all_to_all | solution.py:354
  191.1 1.4 unpack.2
  192.5 24.6 %all-to-all-done.3.in_ref = bf16[8,2,128,512]{3,2,1,0:T(8,128)(2,1)} async-done(((bf16[8,2,128,512]{3,2,1,0:T(8,128)(2,1)}), bf16[8,2,128,512]{3,2,1,0:T(8,128)(2,1)}, u32[]{:S(2)}, u32[]{:S(2)}) %all-to-all-start.3) | async-done | bytes 2097184 | tf_op jit(solution)/shard_map/all_to_all | solution.py:354
  217.1 3.0 %unpack.3 = (bf16[128,4096]{1,0:T(8,128)(2,1)}, bf16[128,4096]{1,0:T(8,128)(2,1)}) custom-call(bf16[8,2,128,512]{3,2,1,0:T(8,128)(2,1)} %all-to-all-done.3.in_ref), custom_call_target="tpu_custom_call" | custom-call | tf_op jit(solution)/shard_map/unpack/pallas_call | solution.py:92
  (71 shorter events, 2.3 us)
Async XLA Ops:
  3.2 5.3 %copy-start.3 = (s32[32,32]{1,0:T(8,128)S(1)}, s32[32,32]{1,0:T(8,128)}, u32[]{:S(2)}) copy-start(s32[32,32]{1,0:T(8,128)} %param.55) | copy-start | bytes 12292
  3.2 31.2 %all-to-all-start.1 = ((bf16[8,2,128,512]{3,2,1,0:T(8,128)(2,1)}), bf16[8,2,128,512]{3,2,1,0:T(8,128)(2,1)S(1)}, u32[]{:S(2)}, u32[]{:S(2)}) async-start(bf16[8,2,128,512]{3,2,1,0:T(8,128)(2,1)} %pack.3), calls=%async_computation.1 | async-start | bytes 4194304 | tf_op jit(solution)/shard_map/all_to_all | solution.py:354
  34.5 4.7 %copy-start.2 = (bf16[8,2,128,512]{3,2,1,0:T(8,128)(2,1)}, bf16[8,2,128,512]{3,2,1,0:T(8,128)(2,1)S(1)}, u32[]{:S(2)}) copy-start(bf16[8,2,128,512]{3,2,1,0:T(8,128)(2,1)S(1)} %all-to-all-done.1.kv_local.kv_ref) | copy-start | bytes 6291460
  34.5 30.4 %all-to-all-start = ((bf16[8,2,128,512]{3,2,1,0:T(8,128)(2,1)}), bf16[8,2,128,512]{3,2,1,0:T(8,128)(2,1)}, u32[]{:S(2)}, u32[]{:S(2)}) async-start(bf16[8,2,128,512]{3,2,1,0:T(8,128)(2,1)} %pack.2), calls=%async_computation | async-start | bytes 4194304 | tf_op jit(solution)/shard_map/all_to_all | solution.py:354
  40.4 26.7 %collective-permute-start.40 = (bf16[4,2,128,512]{3,2,1,0:T(8,128)(2,1)}, bf16[4,2,128,512]{3,2,1,0:T(8,128)(2,1)S(1)}, u32[]{:S(2)}, u32[]{:S(2)}) collective-permute-start(bf16[4,2,128,512]{3,2,1,0:T(8,128)(2,1)} %get-tuple-element.1178), channel_id=1, source_target_pairs={{0,2},{2,4},{4,6},{1,3},{3,5},{5,7},{8,10},{10,12},{12,14},{9,11},... | collective-permute-start | bytes 3145736 | tf_op jit(solution)/shard_map/ppermute | solution.py:369
  43.9 27.1 %collective-permute-start.41 = (bf16[4,2,128,512]{3,2,1,0:T(8,128)(2,1)S(1)}, bf16[4,2,128,512]{3,2,1,0:T(8,128)(2,1)S(1)}, u32[]{:S(2)}, u32[]{:S(2)}) collective-permute-start(bf16[4,2,128,512]{3,2,1,0:T(8,128)(2,1)S(1)} %get-tuple-element.1177), channel_id=1, source_target_pairs={{2,0},{4,2},{6,4},{3,1},{5,3},{7,5},{10,8},{12,10},{14,12},{11,9},... | collective-permute-start | bytes 3145736 | tf_op jit(solution)/shard_map/ppermute | solution.py:370
  49.1 1.7 collective-permute-start.4
  82.6 1.3 copy-start.1
  83.9 102.8 %all-to-all-start.2 = ((bf16[8,2,128,512]{3,2,1,0:T(8,128)(2,1)}), bf16[8,2,128,512]{3,2,1,0:T(8,128)(2,1)S(1)}, u32[]{:S(2)}, u32[]{:S(2)}) async-start(bf16[8,2,128,512]{3,2,1,0:T(8,128)(2,1)} %copy-done.1), calls=%async_computation.2 | async-start | bytes 4194304 | tf_op jit(solution)/shard_map/all_to_all | solution.py:354
  90.8 84.3 %collective-permute-start.45 = (bf16[4,2,128,512]{3,2,1,0:T(8,128)(2,1)}, bf16[4,2,128,512]{3,2,1,0:T(8,128)(2,1)S(1)}, u32[]{:S(2)}, u32[]{:S(2)}) collective-permute-start(bf16[4,2,128,512]{3,2,1,0:T(8,128)(2,1)} %get-tuple-element.1176), channel_id=1, source_target_pairs={{0,2},{2,4},{4,6},{1,3},{3,5},{5,7},{8,10},{10,12},{12,14},{9,11},... | collective-permute-start | bytes 3145736 | tf_op jit(solution)/shard_map/ppermute | solution.py:369
  118.2 56.9 %collective-permute-start.46 = (bf16[4,2,128,512]{3,2,1,0:T(8,128)(2,1)}, bf16[4,2,128,512]{3,2,1,0:T(8,128)(2,1)}, u32[]{:S(2)}, u32[]{:S(2)}) collective-permute-start(bf16[4,2,128,512]{3,2,1,0:T(8,128)(2,1)} %get-tuple-element.1175), channel_id=1, source_target_pairs={{2,0},{4,2},{6,4},{3,1},{5,3},{7,5},{10,8},{12,10},{14,12},{11,9},... | collective-permute-start | bytes 3145736 | tf_op jit(solution)/shard_map/ppermute | solution.py:370
  121.2 1.6 collective-permute-start.24
  123.7 48.1 %collective-permute-start.42 = (f32[8,8,128]{2,1,0:T(8,128)S(1)}, f32[8,8,128]{2,1,0:T(8,128)S(1)}, u32[]{:S(2)}, u32[]{:S(2)}) collective-permute-start(f32[8,8,128]{2,1,0:T(8,128)S(1)} %get-tuple-element.1004), channel_id=1, source_target_pairs={{0,2},{2,0},{4,6},{6,4},{1,3},{3,1},{5,7},{7,5},{8,10},{10,8},{12,... | collective-permute-start | bytes 98312 | tf_op jit(solution)/shard_map/ppermute | solution.py:450
  169.3 4.8 %collective-permute-start.43 = (f32[8,8,128]{2,1,0:T(8,128)S(1)}, f32[8,8,128]{2,1,0:T(8,128)S(1)}, u32[]{:S(2)}, u32[]{:S(2)}) collective-permute-start(f32[8,8,128]{2,1,0:T(8,128)S(1)} %get-tuple-element.1004), channel_id=1, source_target_pairs={{0,4},{2,6},{4,0},{6,2},{1,5},{3,7},{5,1},{7,3},{8,12},{10,14},{12... | collective-permute-start | bytes 98312 | tf_op jit(solution)/shard_map/ppermute | solution.py:450
  169.3 5.7 %collective-permute-start.44 = (f32[8,8,128]{2,1,0:T(8,128)S(1)}, f32[8,8,128]{2,1,0:T(8,128)S(1)}, u32[]{:S(2)}, u32[]{:S(2)}) collective-permute-start(f32[8,8,128]{2,1,0:T(8,128)S(1)} %get-tuple-element.1004), channel_id=1, source_target_pairs={{0,6},{2,4},{4,2},{6,0},{1,7},{3,5},{5,3},{7,1},{8,14},{10,12},{12... | collective-permute-start | bytes 98312 | tf_op jit(solution)/shard_map/ppermute | solution.py:450
  185.4 1.3 copy-start
  186.7 30.4 %all-to-all-start.3 = ((bf16[8,2,128,512]{3,2,1,0:T(8,128)(2,1)}), bf16[8,2,128,512]{3,2,1,0:T(8,128)(2,1)}, u32[]{:S(2)}, u32[]{:S(2)}) async-start(bf16[8,2,128,512]{3,2,1,0:T(8,128)(2,1)} %copy-done), calls=%async_computation.3 | async-start | bytes 4194304 | tf_op jit(solution)/shard_map/all_to_all | solution.py:354

commit v4 on v3

--- a/solution.py
+++ b/solution.py
@@ -241,18 +241,22 @@
 
 
 def patterns_of(steps):
-    groups, index = [], {}
+    groups, sizes, joined = [], [], []
     for d in range(1, steps):
         top = 1 << (d.bit_length() - 1)
         for low in range(top):
             pairs = [a for a in range(steps) if not a & top and a % top == low]
-            for a in pairs:
-                index[a, a ^ d] = index[a ^ d, a] = len(groups)
+            if d == 2:
+                joined.append(len(groups))
             groups.append([(a, a ^ d) for a in pairs] + [(a ^ d, a) for a in pairs])
-    return groups, index
-
-
-def tables(block_mask, spans, span_len, steps, groups):
+            sizes.append((WIDE, WIDE // 2) if d < 3 else (WIDE,))
+    if joined:
+        groups.append(sum((groups[g] for g in joined), []))
+        sizes.append((WIDE // 2,))
+    return groups, sizes, joined
+
+
+def tables(block_mask, spans, span_len, steps, groups, sizes, joined):
     z = lax.axis_index("z")
     local = spans * SUB
     most = (spans * (spans - 1) + (WIDE - 1) * len(groups)) // WIDE
@@ -273,6 +277,15 @@
     per_place = group.reshape(spans, steps, SUB, spans)
     numbers = iota((len(groups), spans, steps, SUB, spans), 0)
     messages = jnp.max(jnp.sum(as_int(per_place[None] == numbers), axis=(1, 3, 4)), axis=1)
+    if joined:
+        one, two = joined
+        small = jnp.maximum(messages[one], messages[two])
+        join = (jnp.minimum(messages[one], messages[two]) > 0) & (small <= WIDE // 2)
+        member = iota(messages.shape, 0)
+        in_pair = (member == one) | (member == two)
+        messages = jnp.where(join & in_pair, 0, messages)
+        messages = jnp.where(join & (member == len(groups) - 1), small, messages)
+        group = jnp.where(join & ((group == one) | (group == two)), len(groups) - 1, group)
     rounds = (messages + WIDE - 1) // WIDE
     number = iota((len(groups), len(groups)), 0)
     ends = jnp.sum(jnp.where(number <= iota(number.shape, 1), rounds[:, None], 0), axis=0)
@@ -283,7 +296,13 @@
     left = jnp.sum(
         jnp.where(plan[:, None] == iota(at.shape, 1), messages[None] - WIDE * (at - starts[None]), 0), axis=1
     )
-    plan = 2 * plan + as_int(left <= WIDE // 2)
+    base = 0
+    move = jnp.zeros_like(plan)
+    for g, allowed in enumerate(sizes):
+        choice = base + (as_int(left <= WIDE // 2) if len(allowed) > 1 else 0)
+        move = jnp.where(plan == g, choice, move)
+        base += len(allowed)
+    plan = move
     key = jnp.where(
         mine < other,
         (mine * span_len + spot) * spans + other,
@@ -348,7 +367,7 @@
     steps = lax.axis_size("z")
     span_len = steps * SUB
     local = spans * SUB
-    groups, _ = patterns_of(steps)
+    groups, sizes, joined = patterns_of(steps)
 
     def exchange(pair):
         return lax.all_to_all(pair, ("blk", "x"), split_axis=0, concat_axis=0, tiled=True)
@@ -357,9 +376,7 @@
     qg = exchange(pack(query_tokens, cotangent, local))
     columns = kv.shape[3]
     heads = columns // HEAD_DIM
-    slot, ok, place, cross, total, plan, capacity = tables(
-        block_mask, spans, span_len, steps, groups
-    )
+    slot, ok, place, cross, total, plan, capacity = tables(block_mask, spans, span_len, steps, groups, sizes, joined)
     width = slot.shape[1]
     upward = [(n, n + 1) for n in range(steps - 1)]
     downward = [(n + 1, n) for n in range(steps - 1)]
@@ -387,8 +404,8 @@
 
     swaps = [
         lambda pair, *picks, g=g, n=n: swap(pair, *picks, group=g, size=n)
-        for g in groups
-        for n in (WIDE, WIDE // 2)
+        for g, allowed in zip(groups, sizes)
+        for n in allowed
     ]
     blank = functools.partial(
         pl.pallas_call,

time: 221 us -> 221 us (level)
  waiting for transfers between devices: 66.6 us -> 63.5 us
  between operations: 2.78 us -> 5.34 us
    all_to_all x4, waiting for transfers between devices: 57.3 us -> 53.9 us  [exchange(): lax.all_to_all(pair, ('blk', 'x'), split_axis=0, concat_axis=0, tiled=True)]
where the time goes in v4:
time: 221 us; the launch traced here: 220 us
  starting transfers between devices  103 us (47%)
  waiting for transfers between devices  63.5 us (29%)
  Pallas kernels  33 us (15%)
  local copies, waits for them, and re-layouts  11 us (5%)
  between operations  5.34 us (2%)
  other arithmetic  3.66 us (2%)
    all_to_all x4, waiting for transfers between devices, exchange(): lax.all_to_all(pair, ('blk', 'x'), split_axis=0, concat_axis=0, tiled=True)  53.9 us
    ppermute x3, starting transfers between devices, shards(): lax.ppermute(stats, 'z', [(n, n ^ d) for n in range(steps)])  48.1 us
    ppermute x2, starting transfers between devices, neighbours(): below = lax.ppermute(edges[:, SUB - 1], 'z', upward)  30.9 us
    all_to_all x4, starting transfers between devices, exchange(): lax.all_to_all(pair, ('blk', 'x'), split_axis=0, concat_axis=0, tiled=True)  17.8 us
    pallas_call x1, Pallas kernels, shards(): pl.pallas_call(functools.partial(key_kernel, width, heads), out_shape=jax...  11.7 us
    pallas_call x1, Pallas kernels, shards(): pl.pallas_call(functools.partial(query_kernel, width, heads), out_shape=(...  11.6 us
    pallas_call x2, Pallas kernels, pack(): pl.pallas_call(pack_kernel, out_shape=jax.ShapeDtypeStruct(shape, a.dtype...  5.28 us
    pallas_call x2, Pallas kernels, unpack(): pl.pallas_call(unpack_kernel, out_shape=(flat, flat), in_specs=[pl.BlockS...  4.47 us
  transfers between devices with their start and end apart: 13, of which 7 were waited for; matrix products, arithmetic and copies ran while one was open for 6% of the time, Pallas kernels for 7%

profile of v4, /device:TPU:0, one launch (start us, length us, event | category | flops | bytes accessed | tf_op | source)
XLA Modules:
  0.0 220.5 jit_solution(6939457677482709768)
XLA Ops:
  0.6 2.6 %pack.3 = bf16[8,2,128,512]{3,2,1,0:T(8,128)(2,1)} custom-call(bf16[128,4096]{1,0:T(8,128)(2,1)} %a_ref.3, bf16[128,4096]{1,0:T(8,128)(2,1)} %b_ref.3), custom_call_target="tpu_custom_call" | custom-call | tf_op jit(solution)/shard_map/pack/pallas_call | solution.py:74
  3.3 5.2 %all-to-all-start.1 = ((bf16[8,2,128,512]{3,2,1,0:T(8,128)(2,1)}), bf16[8,2,128,512]{3,2,1,0:T(8,128)(2,1)S(1)}, u32[]{:S(2)}, u32[]{:S(2)}) async-start(bf16[8,2,128,512]{3,2,1,0:T(8,128)(2,1)} %pack.3), calls=%async_computation.1 | async-start | bytes 4194304 | tf_op jit(solution)/shard_map/all_to_all | solution.py:373
  8.6 0.6 multiply_reduce_fusion
  9.3 0.2 fusion
  9.5 0.2 compare_select_fusion
  9.9 0.6 fusion.37
  13.1 0.6 fusion.34
  14.3 0.2 convert_reduce_fusion.1
  14.9 0.1 copy.75
  15.2 2.7 %pack.2 = bf16[8,2,128,512]{3,2,1,0:T(8,128)(2,1)} custom-call(bf16[128,4096]{1,0:T(8,128)(2,1)} %a_ref.2, bf16[128,4096]{1,0:T(8,128)(2,1)} %b_ref.2), custom_call_target="tpu_custom_call" | custom-call | tf_op jit(solution)/shard_map/pack/pallas_call | solution.py:74
  18.0 0.2 slice_reduce_fusion.3
  18.2 0.2 select_reduce_fusion.4
  18.5 16.0 %all-to-all-done.1.kv_local.kv_ref = bf16[8,2,128,512]{3,2,1,0:T(8,128)(2,1)S(1)} async-done(((bf16[8,2,128,512]{3,2,1,0:T(8,128)(2,1)}), bf16[8,2,128,512]{3,2,1,0:T(8,128)(2,1)S(1)}, u32[]{:S(2)}, u32[]{:S(2)}) %all-to-all-start.1) | async-done | bytes 2097184 | tf_op jit(solution)/shard_map/all_to_all | solution.py:373
  34.5 4.3 %all-to-all-start = ((bf16[8,2,128,512]{3,2,1,0:T(8,128)(2,1)}), bf16[8,2,128,512]{3,2,1,0:T(8,128)(2,1)}, u32[]{:S(2)}, u32[]{:S(2)}) async-start(bf16[8,2,128,512]{3,2,1,0:T(8,128)(2,1)} %pack.2), calls=%async_computation | async-start | bytes 4194304 | tf_op jit(solution)/shard_map/all_to_all | solution.py:373
  38.9 0.1 convert_reduce_fusion.4
  39.0 0.1 copy.72
  39.3 0.1 add_select_fusion.8
  39.4 1.2 slice_bitcast_fusion.2
  40.5 3.5 %collective-permute-start.36 = (bf16[4,2,128,512]{3,2,1,0:T(8,128)(2,1)}, bf16[4,2,128,512]{3,2,1,0:T(8,128)(2,1)S(1)}, u32[]{:S(2)}, u32[]{:S(2)}) collective-permute-start(bf16[4,2,128,512]{3,2,1,0:T(8,128)(2,1)} %get-tuple-element.1127), channel_id=1, source_target_pairs={{0,2},{2,4},{4,6},{1,3},{3,5},{5,7},{8,10},{10,12},{12,14},{9,11},... | collective-permute-start | bytes 3145736 | tf_op jit(solution)/shard_map/ppermute | solution.py:386
  44.1 1.3 collective-permute-start.37
  47.6 3.3 %conditional.4 = (bf16[4,2,128,512]{3,2,1,0:T(8,128)(2,1)}) conditional(s32[]{:T(128)} %clamp.18, bf16[4,2,128,512]{3,2,1,0:T(8,128)(2,1)} %extra_blocks.4, (s32[]{:T(128)}, bf16[8,2,128,512]{3,2,1,0:T(8,128)(2,1)}, s32[]{:T(128)}, s32[]{:T(128)}, s32[]{:T(128)}) %tuple.345, (s32[]{:T(128)}, ...), branch_computations={%region_14.15_spmd, %region_15.16_spmd, %region_16.17_spmd, %regio... | conditional | flops 1572876 | bytes 8388808 | solution.py:431
  47.6 1.5 constant_dynamic-slice_fusion.15
  49.1 0.1 pad_maximum_fusion.6
  49.2 1.7 collective-permute-start.4
  50.9 0.7 while.26
  51.6 13.3 %all-to-all-done.qg_ref.qg_local = bf16[8,2,128,512]{3,2,1,0:T(8,128)(2,1)} async-done(((bf16[8,2,128,512]{3,2,1,0:T(8,128)(2,1)}), bf16[8,2,128,512]{3,2,1,0:T(8,128)(2,1)}, u32[]{:S(2)}, u32[]{:S(2)}) %all-to-all-start) | async-done | bytes 2097184 | tf_op jit(solution)/shard_map/all_to_all | solution.py:373
  64.9 2.4 %collective-permute-done.36.below = bf16[4,2,128,512]{3,2,1,0:T(8,128)(2,1)S(1)} collective-permute-done((bf16[4,2,128,512]{3,2,1,0:T(8,128)(2,1)}, bf16[4,2,128,512]{3,2,1,0:T(8,128)(2,1)S(1)}, u32[]{:S(2)}, u32[]{:S(2)}) %collective-permute-start.36) | collective-permute-done | bytes 1048608 | tf_op jit(solution)/shard_map/ppermute | solution.py:386
  67.3 3.9 %collective-permute-done.37.above = bf16[4,2,128,512]{3,2,1,0:T(8,128)(2,1)S(1)} collective-permute-done((bf16[4,2,128,512]{3,2,1,0:T(8,128)(2,1)S(1)}, bf16[4,2,128,512]{3,2,1,0:T(8,128)(2,1)S(1)}, u32[]{:S(2)}, u32[]{:S(2)}) %collective-permute-start.37) | collective-permute-done | bytes 1048608 | tf_op jit(solution)/shard_map/ppermute | solution.py:387
  71.1 11.6 %query_pass.1 = (bf16[8,2,128,512]{3,2,1,0:T(8,128)(2,1)S(1)}, f32[8,8,128]{2,1,0:T(8,128)S(1)}) custom-call(s32[8,6]{1,0:T(8,128)S(1)} %add_select_fusion.5.slot_ref, s32[8,6]{1,0:T(8,128)S(1)} %get-tuple-element.997.valid_ref, s32[8]{0:T(128)S(1)} %reduce_sum.137.cross_ref, s32[1]{0:T(128)} %bitcast.6.count_ref, ...), custom_call_target="tpu_custom_call" | custom-call | flops 3221225472 | bytes 8388608 | tf_op jit(solution)/shard_map/query_pass/pallas_call | solution.py:454
  82.8 1.4 copy-done
  84.2 3.8 %all-to-all-start.2 = ((bf16[8,2,128,512]{3,2,1,0:T(8,128)(2,1)}), bf16[8,2,128,512]{3,2,1,0:T(8,128)(2,1)S(1)}, u32[]{:S(2)}, u32[]{:S(2)}) async-start(bf16[8,2,128,512]{3,2,1,0:T(8,128)(2,1)} %copy-done), calls=%async_computation.2 | async-start | bytes 4194304 | tf_op jit(solution)/shard_map/all_to_all | solution.py:373
  88.0 3.0 %slice_bitcast_fusion = (bf16[4,2,128,512]{3,2,1,0:T(8,128)(2,1)}, bf16[4,2,128,512]{3,2,1,0:T(8,128)(2,1)}) fusion(bf16[4,2,2,128,512]{4,3,2,1,0:T(8,128)(2,1)} %bitcast.11), kind=kLoop, calls=%fused_computation.166 | loop fusion | bytes 4194304 | tf_op jit(solution)/shard_map/squeeze | solution.py:387
  91.1 27.4 %collective-permute-start.41 = (bf16[4,2,128,512]{3,2,1,0:T(8,128)(2,1)}, bf16[4,2,128,512]{3,2,1,0:T(8,128)(2,1)S(1)}, u32[]{:S(2)}, u32[]{:S(2)}) collective-permute-start(bf16[4,2,128,512]{3,2,1,0:T(8,128)(2,1)} %get-tuple-element.1125), channel_id=1, source_target_pairs={{0,2},{2,4},{4,6},{1,3},{3,5},{5,7},{8,10},{10,12},{12,14},{9,11},... | collective-permute-start | bytes 3145736 | tf_op jit(solution)/shard_map/ppermute | solution.py:386
  118.5 1.3 collective-permute-start.42
  119.8 3.3 %conditional.5 = (bf16[4,2,128,512]{3,2,1,0:T(8,128)(2,1)}) conditional(s32[]{:T(128)} %clamp.18, bf16[4,2,128,512]{3,2,1,0:T(8,128)(2,1)} %extra_blocks.6, (s32[]{:T(128)}, bf16[8,2,128,512]{3,2,1,0:T(8,128)(2,1)}, s32[]{:T(128)}, s32[]{:T(128)}, s32[]{:T(128)}) %tuple.171, (s32[]{:T(128)}, ...), branch_computations={%region_36.37_spmd, %region_37.38_spmd, %region_38.39_spmd, %regio... | conditional | flops 1572876 | bytes 8388808 | solution.py:431
  119.9 1.5 constant_dynamic-slice_fusion.71
  121.3 0.1 pad_maximum_fusion.32
  121.5 1.6 collective-permute-start.22
  123.1 0.7 while.27
  123.8 45.6 %collective-permute-start.38 = (f32[8,8,128]{2,1,0:T(8,128)S(1)}, f32[8,8,128]{2,1,0:T(8,128)S(1)}, u32[]{:S(2)}, u32[]{:S(2)}) collective-permute-start(f32[8,8,128]{2,1,0:T(8,128)S(1)} %get-tuple-element.964), channel_id=1, source_target_pairs={{0,2},{2,0},{4,6},{6,4},{1,3},{3,1},{5,7},{7,5},{8,10},{10,8},{12,... | collective-permute-start | bytes 98312 | tf_op jit(solution)/shard_map/ppermute | solution.py:467
  169.4 2.4 %collective-permute-start.40 = (f32[8,8,128]{2,1,0:T(8,128)S(1)}, f32[8,8,128]{2,1,0:T(8,128)S(1)}, u32[]{:S(2)}, u32[]{:S(2)}) collective-permute-start(f32[8,8,128]{2,1,0:T(8,128)S(1)} %get-tuple-element.964), channel_id=1, source_target_pairs={{0,6},{2,4},{4,2},{6,0},{1,7},{3,5},{5,3},{7,1},{8,14},{10,12},{12... | collective-permute-start | bytes 98312 | tf_op jit(solution)/shard_map/ppermute | solution.py:467
  171.8 2.4 %collective-permute-done.39 = f32[8,8,128]{2,1,0:T(8,128)S(1)} collective-permute-done((f32[8,8,128]{2,1,0:T(8,128)S(1)}, f32[8,8,128]{2,1,0:T(8,128)S(1)}, u32[]{:S(2)}, u32[]{:S(2)}) %collective-permute-start.39) | collective-permute-done | bytes 32800 | tf_op jit(solution)/shard_map/ppermute | solution.py:467
  174.2 0.9 collective-permute-done.40
  175.2 11.7 %key_pass.1 = bf16[8,2,128,512]{3,2,1,0:T(8,128)(2,1)} custom-call(s32[8,6]{1,0:T(8,128)S(1)} %add_select_fusion.5.slot_ref, s32[8,6]{1,0:T(8,128)S(1)} %get-tuple-element.997.valid_ref, s32[8,6]{1,0:T(8,128)S(1)} %get-tuple-element.995.place_ref, s32[8]{0:T(128)S(1)} %reduce_sum.137.cross_ref, s32[1]{0:T(128)} %bitcast.6.count_ref, ...), custom_call_target="tpu_custom_call" | custom-call | flops 3221225472 | bytes 8388608 | tf_op jit(solution)/shard_map/key_pass/pallas_call | solution.py:470
  186.8 4.4 %all-to-all-start.3 = ((bf16[8,2,128,512]{3,2,1,0:T(8,128)(2,1)}), bf16[8,2,128,512]{3,2,1,0:T(8,128)(2,1)}, u32[]{:S(2)}, u32[]{:S(2)}) async-start(bf16[8,2,128,512]{3,2,1,0:T(8,128)(2,1)} %key_pass.1), calls=%async_computation.3 | async-start | bytes 4194304 | tf_op jit(solution)/shard_map/all_to_all | solution.py:373
  191.2 1.4 unpack.2
  192.7 24.6 %all-to-all-done.3.in_ref = bf16[8,2,128,512]{3,2,1,0:T(8,128)(2,1)} async-done(((bf16[8,2,128,512]{3,2,1,0:T(8,128)(2,1)}), bf16[8,2,128,512]{3,2,1,0:T(8,128)(2,1)}, u32[]{:S(2)}, u32[]{:S(2)}) %all-to-all-start.3) | async-done | bytes 2097184 | tf_op jit(solution)/shard_map/all_to_all | solution.py:373
  217.3 3.0 %unpack.3 = (bf16[128,4096]{1,0:T(8,128)(2,1)}, bf16[128,4096]{1,0:T(8,128)(2,1)}) custom-call(bf16[8,2,128,512]{3,2,1,0:T(8,128)(2,1)} %all-to-all-done.3.in_ref), custom_call_target="tpu_custom_call" | custom-call | tf_op jit(solution)/shard_map/unpack/pallas_call | solution.py:92
  (70 shorter events, 2.5 us)
Async XLA Ops:
  3.2 5.3 %copy-start.2 = (s32[32,32]{1,0:T(8,128)S(1)}, s32[32,32]{1,0:T(8,128)}, u32[]{:S(2)}) copy-start(s32[32,32]{1,0:T(8,128)} %param.51) | copy-start | bytes 12292
  3.3 31.2 %all-to-all-start.1 = ((bf16[8,2,128,512]{3,2,1,0:T(8,128)(2,1)}), bf16[8,2,128,512]{3,2,1,0:T(8,128)(2,1)S(1)}, u32[]{:S(2)}, u32[]{:S(2)}) async-start(bf16[8,2,128,512]{3,2,1,0:T(8,128)(2,1)} %pack.3), calls=%async_computation.1 | async-start | bytes 4194304 | tf_op jit(solution)/shard_map/all_to_all | solution.py:373
  34.5 4.9 %copy-start.1 = (bf16[8,2,128,512]{3,2,1,0:T(8,128)(2,1)}, bf16[8,2,128,512]{3,2,1,0:T(8,128)(2,1)S(1)}, u32[]{:S(2)}) copy-start(bf16[8,2,128,512]{3,2,1,0:T(8,128)(2,1)S(1)} %all-to-all-done.1.kv_local.kv_ref) | copy-start | bytes 6291460
  34.5 30.4 %all-to-all-start = ((bf16[8,2,128,512]{3,2,1,0:T(8,128)(2,1)}), bf16[8,2,128,512]{3,2,1,0:T(8,128)(2,1)}, u32[]{:S(2)}, u32[]{:S(2)}) async-start(bf16[8,2,128,512]{3,2,1,0:T(8,128)(2,1)} %pack.2), calls=%async_computation | async-start | bytes 4194304 | tf_op jit(solution)/shard_map/all_to_all | solution.py:373
  40.5 26.7 %collective-permute-start.36 = (bf16[4,2,128,512]{3,2,1,0:T(8,128)(2,1)}, bf16[4,2,128,512]{3,2,1,0:T(8,128)(2,1)S(1)}, u32[]{:S(2)}, u32[]{:S(2)}) collective-permute-start(bf16[4,2,128,512]{3,2,1,0:T(8,128)(2,1)} %get-tuple-element.1127), channel_id=1, source_target_pairs={{0,2},{2,4},{4,6},{1,3},{3,5},{5,7},{8,10},{10,12},{12,14},{9,11},... | collective-permute-start | bytes 3145736 | tf_op jit(solution)/shard_map/ppermute | solution.py:386
  44.1 27.1 %collective-permute-start.37 = (bf16[4,2,128,512]{3,2,1,0:T(8,128)(2,1)S(1)}, bf16[4,2,128,512]{3,2,1,0:T(8,128)(2,1)S(1)}, u32[]{:S(2)}, u32[]{:S(2)}) collective-permute-start(bf16[4,2,128,512]{3,2,1,0:T(8,128)(2,1)S(1)} %get-tuple-element.1126), channel_id=1, source_target_pairs={{2,0},{4,2},{6,4},{3,1},{5,3},{7,5},{10,8},{12,10},{14,12},{11,9},... | collective-permute-start | bytes 3145736 | tf_op jit(solution)/shard_map/ppermute | solution.py:387
  49.2 1.7 collective-permute-start.4
  82.8 1.4 copy-start
  84.2 102.6 %all-to-all-start.2 = ((bf16[8,2,128,512]{3,2,1,0:T(8,128)(2,1)}), bf16[8,2,128,512]{3,2,1,0:T(8,128)(2,1)S(1)}, u32[]{:S(2)}, u32[]{:S(2)}) async-start(bf16[8,2,128,512]{3,2,1,0:T(8,128)(2,1)} %copy-done), calls=%async_computation.2 | async-start | bytes 4194304 | tf_op jit(solution)/shard_map/all_to_all | solution.py:373
  91.1 84.1 %collective-permute-start.41 = (bf16[4,2,128,512]{3,2,1,0:T(8,128)(2,1)}, bf16[4,2,128,512]{3,2,1,0:T(8,128)(2,1)S(1)}, u32[]{:S(2)}, u32[]{:S(2)}) collective-permute-start(bf16[4,2,128,512]{3,2,1,0:T(8,128)(2,1)} %get-tuple-element.1125), channel_id=1, source_target_pairs={{0,2},{2,4},{4,6},{1,3},{3,5},{5,7},{8,10},{10,12},{12,14},{9,11},... | collective-permute-start | bytes 3145736 | tf_op jit(solution)/shard_map/ppermute | solution.py:386
  118.5 56.7 %collective-permute-start.42 = (bf16[4,2,128,512]{3,2,1,0:T(8,128)(2,1)}, bf16[4,2,128,512]{3,2,1,0:T(8,128)(2,1)}, u32[]{:S(2)}, u32[]{:S(2)}) collective-permute-start(bf16[4,2,128,512]{3,2,1,0:T(8,128)(2,1)} %get-tuple-element.1124), channel_id=1, source_target_pairs={{2,0},{4,2},{6,4},{3,1},{5,3},{7,5},{10,8},{12,10},{14,12},{11,9},... | collective-permute-start | bytes 3145736 | tf_op jit(solution)/shard_map/ppermute | solution.py:387
  121.5 1.6 collective-permute-start.22
  123.8 48.1 %collective-permute-start.38 = (f32[8,8,128]{2,1,0:T(8,128)S(1)}, f32[8,8,128]{2,1,0:T(8,128)S(1)}, u32[]{:S(2)}, u32[]{:S(2)}) collective-permute-start(f32[8,8,128]{2,1,0:T(8,128)S(1)} %get-tuple-element.964), channel_id=1, source_target_pairs={{0,2},{2,0},{4,6},{6,4},{1,3},{3,1},{5,7},{7,5},{8,10},{10,8},{12,... | collective-permute-start | bytes 98312 | tf_op jit(solution)/shard_map/ppermute | solution.py:467
  169.4 4.8 %collective-permute-start.39 = (f32[8,8,128]{2,1,0:T(8,128)S(1)}, f32[8,8,128]{2,1,0:T(8,128)S(1)}, u32[]{:S(2)}, u32[]{:S(2)}) collective-permute-start(f32[8,8,128]{2,1,0:T(8,128)S(1)} %get-tuple-element.964), channel_id=1, source_target_pairs={{0,4},{2,6},{4,0},{6,2},{1,5},{3,7},{5,1},{7,3},{8,12},{10,14},{12... | collective-permute-start | bytes 98312 | tf_op jit(solution)/shard_map/ppermute | solution.py:467
  169.4 5.7 %collective-permute-start.40 = (f32[8,8,128]{2,1,0:T(8,128)S(1)}, f32[8,8,128]{2,1,0:T(8,128)S(1)}, u32[]{:S(2)}, u32[]{:S(2)}) collective-permute-start(f32[8,8,128]{2,1,0:T(8,128)S(1)} %get-tuple-element.964), channel_id=1, source_target_pairs={{0,6},{2,4},{4,2},{6,0},{1,7},{3,5},{5,3},{7,1},{8,14},{10,12},{12... | collective-permute-start | bytes 98312 | tf_op jit(solution)/shard_map/ppermute | solution.py:467
  186.8 30.4 %all-to-all-start.3 = ((bf16[8,2,128,512]{3,2,1,0:T(8,128)(2,1)}), bf16[8,2,128,512]{3,2,1,0:T(8,128)(2,1)}, u32[]{:S(2)}, u32[]{:S(2)}) async-start(bf16[8,2,128,512]{3,2,1,0:T(8,128)(2,1)} %key_pass.1), calls=%async_computation.3 | async-start | bytes 4194304 | tf_op jit(solution)/shard_map/all_to_all | solution.py:373
